TPU v7x, 32 devices: a whole 2x2x4 slice. The times are simulated.
32 devices in a mesh: dp: 8 (over z, y), tensor: 4 (over x, core).
Axes of the slice: x: 2, y: 2, z: 4, core: 2. Of those that a mesh axis runs over, the one named last changes fastest.
Arguments:
- tokens: bfloat16 [8, 2048, 2048], P(None, 'dp', 'tensor'), may hold values from -6 to 6
- cotangent: bfloat16 [8, 2048, 2048], P(None, 'dp', 'tensor'), may hold values from -6 to 6
- lengths: int32 [8], replicated, may hold values from 1 to 2048, 9830 in all
- w_query: bfloat16 [2048, 2048], P(None, 'tensor'), may hold values from -0.125 to 0.125
- w_key: bfloat16 [2048, 2048], P(None, 'tensor'), may hold values from -0.125 to 0.125
- w_value: bfloat16 [2048, 2048], P(None, 'tensor'), may hold values from -0.125 to 0.125
- w_gate: bfloat16 [2048, 2048], P(None, 'tensor'), may hold values from -0.125 to 0.125
- w_out: bfloat16 [2048, 2048], P('tensor'), may hold values from -0.125 to 0.125
- w_glu_in: bfloat16 [2048, 2, 5632], P(None, None, 'tensor'), may hold values from -0.125 to 0.125
- w_glu_out: bfloat16 [5632, 2048], P('tensor'), may hold values from -0.078125 to 0.078125
Outputs:
- output: bfloat16 [8, 2048, 2048], P(None, 'dp', 'tensor')
- input_grad: bfloat16 [8, 2048, 2048], P(None, 'dp', 'tensor')
- grad_query: float32 [2048, 2048], P('dp', 'tensor')
- grad_key: float32 [2048, 2048], P('dp', 'tensor')
- grad_value: float32 [2048, 2048], P('dp', 'tensor')
- grad_gate: float32 [2048, 2048], P('dp', 'tensor')
- grad_out: float32 [2048, 2048], P('tensor', 'dp')
- grad_glu_in: float32 [2048, 2, 5632], P('dp', None, 'tensor')
- grad_glu_out: float32 [5632, 2048], P('tensor', 'dp')
- rms_values: float32 [3], replicated
Inputs may be any that keep to these rules, and one draw needn't show every extreme that they name: Every sequence has at least one valid token and the longest has exactly 2048; the lengths add up to three fifths of 16384, rounded down.
All inputs are finite; a program needn't handle non-finite values.
Results may differ from a plain program's by a relative error of at most 0.019.
Values may be sent and summed in bfloat16 or wider, within the bound.
No kernel may reach another device: no remote copies, remote signals or barrier semaphores. Data moves between devices by JAX's collectives and lax.ppermute only.
A program may use at most 320 MiB of HBM per device.

v0:
```python
import jax
import jax.numpy as jnp
from jax import lax
from jax.sharding import PartitionSpec as P

D = 2048
HEADS = 16
HEAD_DIM = 128
BLOCK = 256


EPSILON = 1e-06
HIGHEST = lax.Precision.HIGHEST
NARROW = jnp.bfloat16
FLOAT = jnp.float32


def decay_tables(first_head, local_heads, block_count):
    head_ids = (first_head + jnp.arange(local_heads, dtype=jnp.int32)).astype(FLOAT)
    slopes = jnp.exp2(-8.0 * (head_ids + 1.0) / HEADS)
    places = jnp.arange(BLOCK).astype(FLOAT)
    distance = places[:, None] - places[None, :]
    inside = jnp.where(
        distance >= 0, jnp.exp(-slopes[:, None, None] * jnp.maximum(distance, 0.0)), 0.0
    )
    start_decay = jnp.exp(-slopes[None, :] * (places[:, None] + 1.0))
    finish = jnp.exp(-slopes[None, :] * (BLOCK - 1.0 - places[:, None]))
    block_ids = jnp.arange(block_count).astype(FLOAT)
    block_gap = block_ids[:, None] - 1.0 - block_ids[None, :]
    across = jnp.where(
        block_gap >= 0, jnp.exp(-slopes[:, None, None] * BLOCK * jnp.maximum(block_gap, 0.0)), 0.0
    )
    return (inside, start_decay, finish, across)


def row_totals(values):
    return lax.psum(values, "tensor")


def to_shards(partial_value):
    return lax.psum_scatter(partial_value, "tensor", scatter_dimension=1, tiled=True)


def full_rows(values):
    return lax.all_gather(values, "tensor", axis=1, tiled=True)


def contract_rows(left, right):
    return lax.dot_general(left, right, (((0,), (0,)), ((), ())), preferred_element_type=FLOAT)


def contract_cols(left, right):
    return lax.dot_general(left, right, (((1,), (1,)), ((), ())), preferred_element_type=FLOAT)


def rms_scale(values):
    return lax.rsqrt(row_totals(jnp.sum(values * values, axis=1, keepdims=True)) / D + EPSILON)


def norm_back(grad_norm, normed, inverse):
    inner = row_totals(jnp.sum(grad_norm * normed, axis=1, keepdims=True))
    return inverse * (grad_norm - normed * inner / D)


def silu_slope(values):
    sigmoid_part = jax.nn.sigmoid(values)
    return sigmoid_part * (1.0 + values * (1.0 - sigmoid_part))


def project(normed, matrices):
    gathered = lax.all_gather(normed, "tensor", axis=1, tiled=True)
    return (
        [jnp.dot(gathered, matrix, preferred_element_type=FLOAT) for matrix in matrices],
        gathered,
    )


def weight_terms(kept_rows, gradients):
    return [contract_rows(kept_rows, grad_cols) for grad_cols in gradients]


def attend_forward(queries, key_rows, value_rows, tables, block_shape):
    inside, start_decay, finish, across = tables
    query_blocks = queries.reshape(block_shape)
    key_blocks = key_rows.reshape(block_shape)
    value_blocks = value_rows.reshape(block_shape)
    raw_scores = jnp.einsum(
        "snihd,snjhd->snhij", query_blocks, key_blocks, preferred_element_type=FLOAT
    )
    weights = (raw_scores * inside).astype(NARROW)
    near_part = jnp.einsum(
        "snhij,snjhd->snihd", weights, value_blocks, preferred_element_type=FLOAT
    )
    keyed_rows = (key_blocks * finish[:, :, None]).astype(NARROW)
    update = jnp.einsum(
        "snjhd,snjhe->snhde", keyed_rows, value_blocks, preferred_element_type=FLOAT
    )
    carried = jnp.einsum("hbc,schde->sbhde", across, update, precision=HIGHEST).astype(NARROW)
    far_part = jnp.einsum("snihd,snhde->snihe", query_blocks, carried, preferred_element_type=FLOAT)
    return (near_part + far_part * start_decay[:, :, None], (weights, keyed_rows, carried))


def attend_backward(grad_mix, queries, key_rows, value_rows, stored, tables, block_shape):
    inside, start_decay, finish, across = tables
    weights, keyed_rows, carried = stored
    query_blocks = queries.reshape(block_shape)
    key_blocks = key_rows.reshape(block_shape)
    value_blocks = value_rows.reshape(block_shape)
    grad_blocks = grad_mix.reshape(block_shape)
    grad_scores = (
        jnp.einsum("snihd,snjhd->snhij", grad_blocks, value_blocks, preferred_element_type=FLOAT)
        * inside
    ).astype(NARROW)
    grad_values = jnp.einsum(
        "snhij,snihd->snjhd", weights, grad_blocks, preferred_element_type=FLOAT
    )
    grad_queries = jnp.einsum(
        "snhij,snjhd->snihd", grad_scores, key_blocks, preferred_element_type=FLOAT
    )
    grad_keys = jnp.einsum(
        "snhij,snihd->snjhd", grad_scores, query_blocks, preferred_element_type=FLOAT
    )
    grad_far = (grad_blocks * start_decay[:, :, None]).astype(NARROW)
    grad_queries = grad_queries + jnp.einsum(
        "snihe,snhde->snihd", grad_far, carried, preferred_element_type=FLOAT
    )
    grad_state = jnp.einsum(
        "snihd,snihe->snhde", query_blocks, grad_far, preferred_element_type=FLOAT
    )
    grad_update = jnp.einsum("hbc,sbhde->schde", across, grad_state, precision=HIGHEST).astype(
        NARROW
    )
    grad_keyed = jnp.einsum(
        "snjhe,snhde->snjhd", value_blocks, grad_update, preferred_element_type=FLOAT
    )
    grad_values = grad_values + jnp.einsum(
        "snjhd,snhde->snjhe", keyed_rows, grad_update, preferred_element_type=FLOAT
    )
    grad_keys = grad_keys + grad_keyed * finish[:, :, None]
    flat_shape = (queries.shape[0], queries.shape[1])
    return (
        grad_queries.reshape(flat_shape),
        grad_keys.reshape(flat_shape),
        grad_values.reshape(flat_shape),
    )


def output_branch(gated_out, w_out):
    return lax.psum_scatter(
        jnp.dot(gated_out, w_out, preferred_element_type=FLOAT),
        "tensor",
        scatter_dimension=1,
        tiled=True,
    )


def local(tokens, cotangent, lengths, w_query, w_key, w_value, w_gate, w_out, w_glu_in, w_glu_out):
    seq_dev = tokens.shape[0] // lax.axis_size("dp")
    span_len = tokens.shape[1] * lax.axis_size("dp")
    local_width = tokens.shape[2]
    row_count = seq_dev * span_len
    arrived, arrived_cot = (
        lax.all_to_all(tokens, "dp", split_axis=0, concat_axis=1, tiled=True),
        lax.all_to_all(cotangent, "dp", split_axis=0, concat_axis=1, tiled=True),
    )
    my_lengths = lax.dynamic_slice_in_dim(lengths, lax.axis_index("dp") * seq_dev, seq_dev)
    positions = jnp.arange(span_len, dtype=jnp.int32)
    validity = (positions[None, :] < my_lengths[:, None]).astype(FLOAT).reshape(row_count, 1)
    inputs = arrived.reshape(row_count, local_width).astype(FLOAT)
    cot_local = (arrived_cot.reshape(row_count, local_width).astype(FLOAT) * validity).astype(
        NARROW
    )
    inverse_one = rms_scale(inputs)
    normed_one = inputs * inverse_one
    attn_in, kept_one = project(normed_one.astype(NARROW), [w_query, w_key, w_value, w_gate])
    query_pre, key_pre, value_pre, gate_pre = attn_in
    queries = jax.nn.silu(query_pre).astype(NARROW)
    key_rows = jax.nn.silu(key_pre).astype(NARROW)
    value_rows = value_pre.astype(NARROW)
    local_heads = local_width // HEAD_DIM
    block_count = span_len // BLOCK
    block_shape = (seq_dev, block_count, BLOCK, local_heads, HEAD_DIM)
    tables = decay_tables(lax.axis_index("tensor") * local_heads, local_heads, block_count)
    mixture, stored = attend_forward(queries, key_rows, value_rows, tables, block_shape)
    mixture = mixture.reshape(row_count, local_width)
    inverse_mix = rms_scale(mixture)
    normed_mix = mixture * inverse_mix
    gated_out = (normed_mix * gate_pre).astype(NARROW)
    attn_out = output_branch(gated_out, w_out)
    residual = inputs + attn_out
    inverse_two = rms_scale(residual)
    normed_two = residual * inverse_two
    glu_weights = w_glu_in.reshape(D, -1)
    glu_list, kept_two = project(normed_two.astype(NARROW), [glu_weights])
    both_pre = glu_list[0]
    ff_local = w_glu_out.shape[0]
    gate_half = both_pre[:, :ff_local]
    up_half = both_pre[:, ff_local:]
    hidden = (gate_half * up_half).astype(NARROW)
    glu_out = to_shards(jnp.dot(hidden, w_glu_out, preferred_element_type=FLOAT))
    output = (validity * (residual + glu_out)).astype(NARROW)
    local_sums = jnp.stack(
        [
            jnp.sum(validity * residual * residual),
            jnp.sum(validity * attn_out * attn_out),
            jnp.sum(validity * glu_out * glu_out),
        ]
    )
    totals = lax.psum(local_sums, ("dp", "tensor"))
    token_count = jnp.sum(lengths).astype(FLOAT)
    rms_values = jnp.sqrt(totals / (token_count * D) + EPSILON)
    cot_full = full_rows(cot_local)
    grad_hidden = contract_cols(cot_full, w_glu_out)
    grad_both = jnp.concatenate([grad_hidden * up_half, grad_hidden * gate_half], axis=1).astype(
        NARROW
    )
    grad_norm_two = to_shards(contract_cols(grad_both, glu_weights))
    grad_resid = cot_local.astype(FLOAT) + norm_back(grad_norm_two, normed_two, inverse_two)
    glu_term = weight_terms(kept_two, [grad_both])[0]
    down_term = contract_rows(cot_full, hidden)
    grad_full = full_rows(grad_resid.astype(NARROW))
    grad_gated = contract_cols(grad_full, w_out)
    out_term = contract_rows(grad_full, gated_out)
    grad_gate_pre = (grad_gated * normed_mix).astype(NARROW)
    grad_mix = norm_back(grad_gated * gate_pre, normed_mix, inverse_mix).astype(NARROW)
    grad_queries, grad_keys, grad_values = attend_backward(
        grad_mix, queries, key_rows, value_rows, stored, tables, block_shape
    )
    grad_query_pre = (grad_queries * silu_slope(query_pre)).astype(NARROW)
    grad_key_pre = (grad_keys * silu_slope(key_pre)).astype(NARROW)
    grad_value_pre = grad_values.astype(NARROW)
    partial_one = contract_cols(grad_query_pre, w_query) + contract_cols(grad_key_pre, w_key)
    partial_one = (
        partial_one + contract_cols(grad_value_pre, w_value) + contract_cols(grad_gate_pre, w_gate)
    )
    grad_norm_one = to_shards(partial_one)
    input_grad = (grad_resid + norm_back(grad_norm_one, normed_one, inverse_one)).astype(NARROW)
    attn_terms = weight_terms(
        kept_one, [grad_query_pre, grad_key_pre, grad_value_pre, grad_gate_pre]
    )
    query_part, key_part, value_part, gate_part, out_part, glu_part, down_part = (
        lax.psum_scatter(
            attn_terms[0].astype(jnp.bfloat16), "dp", scatter_dimension=0, tiled=True
        ).astype(jnp.float32),
        lax.psum_scatter(
            attn_terms[1].astype(jnp.bfloat16), "dp", scatter_dimension=0, tiled=True
        ).astype(jnp.float32),
        lax.psum_scatter(
            attn_terms[2].astype(jnp.bfloat16), "dp", scatter_dimension=0, tiled=True
        ).astype(jnp.float32),
        lax.psum_scatter(
            attn_terms[3].astype(jnp.bfloat16), "dp", scatter_dimension=0, tiled=True
        ).astype(jnp.float32),
        lax.psum_scatter(
            out_term.astype(jnp.bfloat16), "dp", scatter_dimension=0, tiled=True
        ).astype(jnp.float32),
        lax.psum_scatter(
            glu_term.astype(jnp.bfloat16), "dp", scatter_dimension=0, tiled=True
        ).astype(jnp.float32),
        lax.psum_scatter(
            down_term.astype(jnp.bfloat16), "dp", scatter_dimension=0, tiled=True
        ).astype(jnp.float32),
    )
    output_seq = output.reshape(seq_dev, span_len, local_width)
    input_seq = input_grad.reshape(seq_dev, span_len, local_width)
    returned, returned_grad = (
        lax.all_to_all(output_seq, "dp", split_axis=1, concat_axis=0, tiled=True),
        lax.all_to_all(input_seq, "dp", split_axis=1, concat_axis=0, tiled=True),
    )
    return (
        returned,
        returned_grad,
        query_part,
        key_part,
        value_part,
        gate_part,
        out_part.T,
        glu_part.reshape(glu_part.shape[0], 2, ff_local),
        down_part.T,
        rms_values,
    )


def solution(mesh):
    in_specs = (
        P(None, "dp", "tensor"),
        P(None, "dp", "tensor"),
        P(),
        P(None, "tensor"),
        P(None, "tensor"),
        P(None, "tensor"),
        P(None, "tensor"),
        P("tensor", None),
        P(None, None, "tensor"),
        P("tensor", None),
    )
    out_specs = (
        P(None, "dp", "tensor"),
        P(None, "dp", "tensor"),
        P("dp", "tensor"),
        P("dp", "tensor"),
        P("dp", "tensor"),
        P("dp", "tensor"),
        P("tensor", "dp"),
        P("dp", None, "tensor"),
        P("tensor", "dp"),
        P(),
    )
    return jax.shard_map(local, mesh=mesh, in_specs=in_specs, out_specs=out_specs, check_vma=False)
```

profile of v0, /device:TPU:0, one launch (start us, length us, event | category | flops | bytes accessed | tf_op | source)
XLA Modules:
  0.0 1876.7 jit_solution(9222637776072009716)
XLA Ops:
  7.2 55.8 %all_to_all.42 = bf16[8,256,512]{2,1,0:T(8,128)(2,1)} all-to-all(bf16[8,256,512]{2,1,0:T(8,128)(2,1)} %param.10), channel_id=1, replica_groups=mesh['dp'=8,'tensor'=4] {'dp'}, dimensions={0} | all-to-all | bytes 4194304 | tf_op jit(solution)/shard_map/all_to_all | solution.py:163
  80.5 56.8 %all-gather.5.cloned.1.call-done = bf16[2048,2048]{0,1:T(8,128)(2,1)} async-done(((bf16[2048,512]{0,1:T(8,128)(2,1)}), bf16[2048,2048]{0,1:T(8,128)(2,1)}) %all-gather.5.cloned.1.call-update) | async-done | bytes 8388624 | tf_op jit(solution)/shard_map/all_gather | solution.py:71
  137.3 11.7 multiply_convert_fusion.13
  157.5 11.7 multiply_convert_fusion.12
  173.1 9.9 convolution_convert_fusion.7
  212.9 11.9 multiply_convert_fusion.10
  226.1 8.2 fusion.59
  234.4 126.2 %reduce-scatter.12.cloned.1.call-done = f32[2048,512]{0,1:T(8,128)} async-done(((f32[2048,2048]{0,1:T(8,128)}), f32[2048,512]{0,1:T(8,128)}) %reduce-scatter.12.cloned.1.call-update) | async-done | bytes 4194320 | tf_op jit(solution)/shard_map/reduce_scatter | solution.py:149
  384.9 46.7 %all-to-all-done.2 = bf16[8,256,512]{2,1,0:T(8,128)(2,1)} async-done(((bf16[8,256,512]{2,1,0:T(8,128)(2,1)}), bf16[8,256,512]{2,1,0:T(8,128)(2,1)}, u32[]{:S(2)}, u32[]{:S(2)}) %all-to-all-start.2) | async-done | bytes 2097184 | tf_op jit(solution)/shard_map/all_to_all | solution.py:164
  445.5 11.8 copy.192
  457.3 32.3 %fusion.60 = f32[2048,2816]{1,0:T(8,128)} fusion(bf16[2048,2048]{0,1:T(8,128)(2,1)} %all-gather.7.cloned.1.call-done, bf16[2048,2816]{1,0:T(8,128)(2,1)} %bitcast.178), kind=kOutput, calls=%fused_computation.119 | convolution fusion | flops 23622320128 | bytes 42991616 | tf_op jit(solution)/shard_map/dot_general | solution.py:73
  489.6 12.3 all-gather.9.cloned.1.call-done
  501.9 23.8 %multiply_convert_fusion.1 = (bf16[2048,1408]{1,0:T(8,128)(2,1)}, bf16[2048,1408]{1,0:T(8,128)(2,1)}, bf16[2048,1408]{1,0:T(8,128)(2,1)S(1)}) fusion(f32[2048,2816]{1,0:T(8,128)} %fusion.60, bf16[2048,2048]{0,1:T(8,128)(2,1)} %all-gather.9.cloned.1.call-done, bf16[1408,2048]{1,0:T(8,128)(2,1)} %param.19), kind=kOutput, calls=%fused_computation.3 | convolution fusion | flops 11828461568 | bytes 54525952 | tf_op jit(solution)/shard_map/dot_general | solution.py:53
  528.3 19.3 %fusion.61 = f32[2048,2048]{0,1:T(8,128)} fusion(bf16[2048,1408]{1,0:T(8,128)(2,1)S(1)} %get-tuple-element.60, bf16[1408,2048]{1,0:T(8,128)(2,1)} %param.19), kind=kOutput, calls=%fused_computation.120 | convolution fusion | flops 11811160064 | bytes 28311552 | tf_op jit(solution)/shard_map/dot_general | solution.py:200
  547.6 32.0 %fusion = f32[2048,2048]{0,1:T(8,128)} fusion(bf16[2048,2816]{1,0:T(8,128)(2,1)} %bitcast.179, bf16[2048,1408]{1,0:T(8,128)(2,1)} %get-tuple-element.59, bf16[2048,1408]{1,0:T(8,128)(2,1)} %get-tuple-element.58), kind=kOutput, calls=%fused_computation.9 | convolution fusion | flops 23645388800 | bytes 39845888 | tf_op jit(solution)/shard_map/dot_general | solution.py:53
  579.6 93.1 %reduce-scatter.14.cloned.1.call-done = f32[2048,512]{0,1:T(8,128)} async-done(((f32[2048,2048]{0,1:T(8,128)}), f32[2048,512]{0,1:T(8,128)}) %reduce-scatter.14.cloned.1.call-update) | async-done | bytes 4194320 | tf_op jit(solution)/shard_map/reduce_scatter | solution.py:41
  672.7 127.5 %reduce-scatter.16.cloned.1.call-done = f32[2048,512]{0,1:T(8,128)} async-done(((f32[2048,2048]{0,1:T(8,128)}), f32[2048,512]{0,1:T(8,128)}) %reduce-scatter.16.cloned.1.call-update) | async-done | bytes 4194320 | tf_op jit(solution)/shard_map/reduce_scatter | solution.py:41
  800.3 9.2 fusion.1
  815.3 7.6 fusion.23
  823.0 59.0 %all-gather.11.cloned.1.call-done = bf16[2048,2048]{0,1:T(8,128)(2,1)} async-done(((bf16[2048,512]{0,1:T(8,128)(2,1)}), bf16[2048,2048]{0,1:T(8,128)(2,1)}) %all-gather.11.cloned.1.call-update) | async-done | bytes 8388624 | tf_op jit(solution)/shard_map/all_gather | solution.py:45
  882.0 11.4 multiply_reduce_fusion.1
  945.0 8.5 fusion.64
  966.4 8.1 fusion.62
  977.6 8.3 fusion.66
  985.9 23.7 %add_add_fusion = f32[2048,2048]{0,1:T(8,128)} fusion(f32[2048,2048]{0,1:T(8,128)} %fusion.66, f32[2048,2048]{0,1:T(8,128)} %fusion.62, f32[2048,2048]{0,1:T(8,128)} %fusion.64, bf16[2048,512]{1,0:T(8,128)(2,1)S(1)} %copy-done.20, bf16[2048,512]{0,1:T(8,128)(2,1)S(1)} %copy-done.21), kind=kOutput, calls=%fused_computation | convolution fusion | flops 4307550208 | bytes 71303168 | tf_op jit(solution)/shard_map/dot_general | solution.py:53
  1009.7 18.6 convolution_convert_fusion.1
  1028.4 33.6 %convolution_convert_fusion = bf16[2048,2816]{1,0:T(8,128)(2,1)} fusion(bf16[2048,2048]{0,1:T(8,128)(2,1)} %all-gather.7.cloned.1.call-done, bf16[2048,1408]{1,0:T(8,128)(2,1)} %get-tuple-element.59, bf16[2048,1408]{1,0:T(8,128)(2,1)} %get-tuple-element.58), kind=kOutput, calls=%fused_computation.5 | convolution fusion | flops 23651155968 | bytes 31457280 | tf_op jit(solution)/shard_map/dot_general | solution.py:49
  1062.0 10.3 convolution_convert_fusion.2
  1072.4 9.6 convolution_convert_fusion.5
  1082.0 10.0 convolution_convert_fusion.6
  1092.1 10.0 convolution_convert_fusion.4
  1102.2 8.0 copy.145
  1110.7 14.1 reduce.5
  1134.4 10.0 convolution_convert_fusion.3
  1155.4 9.9 fusion.9
  1165.3 10.7 copy.169
  1176.0 15.4 reduce.6
  1197.7 21.8 %all-to-all-done.1 = bf16[8,2,65536]{2,1,0:T(2,128)(2,1)S(1)} async-done(((bf16[8,2,65536]{2,1,0:T(2,128)(2,1)}), bf16[8,2,65536]{2,1,0:T(2,128)(2,1)S(1)}, u32[]{:S(2)}, u32[]{:S(2)}) %all-to-all-start.1) | async-done | bytes 2097184 | tf_op jit(solution)/shard_map/all_to_all | solution.py:267
  1219.5 7.2 all-to-all-start.3
  1228.0 78.4 %reduce-scatter.32.cloned.1.call-done = bf16[256,1408]{1,0:T(8,128)(2,1)} async-done(((bf16[2048,1408]{1,0:T(8,128)(2,1)}), bf16[256,1408]{1,0:T(8,128)(2,1)}) %reduce-scatter.32.cloned.1.call-update) | async-done | bytes 720912 | tf_op jit(solution)/shard_map/reduce_scatter | solution.py:260
  1311.2 190.8 %reduce-scatter.30.cloned.1.call-done = bf16[256,2816]{1,0:T(8,128)(2,1)} async-done(((bf16[2048,2816]{1,0:T(8,128)(2,1)}), bf16[256,2816]{1,0:T(8,128)(2,1)}) %reduce-scatter.30.cloned.1.call-update) | async-done | bytes 1441808 | tf_op jit(solution)/shard_map/reduce_scatter | solution.py:257
  1506.4 39.8 %psum.55 = f32[3]{0:T(128)S(1)} all-reduce(f32[3]{0:T(128)S(1)} %pad_maximum_fusion.3), channel_id=1, replica_groups=mesh['dp'=8,'tensor'=4] {'dp','tensor'}, use_global_device_ids=true, to_apply=%region_26.27 | all-reduce | flops 3 | bytes 24 | tf_op jit(solution)/shard_map/psum | solution.py:209
  1555.2 18.5 reduce-scatter.28.cloned.1.call-done
  1575.6 68.9 %reduce-scatter.22.cloned.1.call-done = bf16[256,512]{1,0:T(8,128)(2,1)} async-done(((bf16[2048,512]{1,0:T(8,128)(2,1)}), bf16[256,512]{1,0:T(8,128)(2,1)}) %reduce-scatter.22.cloned.1.call-update) | async-done | bytes 262160 | tf_op jit(solution)/shard_map/reduce_scatter | solution.py:245
  1646.4 69.3 %reduce-scatter.20.cloned.1.call-done = bf16[256,512]{1,0:T(8,128)(2,1)} async-done(((bf16[2048,512]{1,0:T(8,128)(2,1)}), bf16[256,512]{1,0:T(8,128)(2,1)}) %reduce-scatter.20.cloned.1.call-update) | async-done | bytes 262160 | tf_op jit(solution)/shard_map/reduce_scatter | solution.py:242
  1717.4 69.1 %reduce-scatter.24.cloned.1.call-done = bf16[256,512]{1,0:T(8,128)(2,1)} async-done(((bf16[2048,512]{1,0:T(8,128)(2,1)}), bf16[256,512]{1,0:T(8,128)(2,1)}) %reduce-scatter.24.cloned.1.call-update) | async-done | bytes 262160 | tf_op jit(solution)/shard_map/reduce_scatter | solution.py:248
  1788.4 68.8 %reduce-scatter.26.cloned.1.call-done = bf16[256,512]{1,0:T(8,128)(2,1)} async-done(((bf16[2048,512]{1,0:T(8,128)(2,1)}), bf16[256,512]{1,0:T(8,128)(2,1)}) %reduce-scatter.26.cloned.1.call-update) | async-done | bytes 262160 | tf_op jit(solution)/shard_map/reduce_scatter | solution.py:251
  1859.0 6.9 reshape.392
  (227 shorter events, 234.7 us)
Async XLA Ops:
  7.2 218.9 %copy-start = (bf16[512,2048]{1,0:T(8,128)(2,1)S(1)}, bf16[512,2048]{1,0:T(8,128)(2,1)}, u32[]{:S(2)}) copy-start(bf16[512,2048]{1,0:T(8,128)(2,1)} %param.17) | copy-start | bytes 6291460
  7.2 130.1 %all-gather.5.cloned.1.call-start = ((), (), s32[]{:S(2)}) async-start(), calls=%async_computation.15 | async-start | bytes 10485760 | tf_op jit(solution)/shard_map/all_gather | solution.py:71
  79.7 280.9 %reduce-scatter.12.cloned.1.call-start = ((), (), s32[]{:S(2)}) async-start(), calls=%async_computation.16 | async-start | bytes 20971520 | tf_op jit(solution)/shard_map/reduce_scatter | solution.py:149
  79.8 116.3 %copy-start.46 = (f32[4]{0:T(128)}, f32[4]{0:T(128)S(1)}, u32[]{:S(2)}) copy-start(f32[4]{0:T(128)S(1)} %broadcast_multiply_fusion) | copy-start | bytes 52
  79.9 116.2 %copy-start.44 = (pred[8,8]{0,1:T(8,128)(4,1)}, pred[8,8]{0,1:T(8,128)(4,1)S(1)}, u32[]{:S(2)}) copy-start(pred[8,8]{0,1:T(8,128)(4,1)S(1)} %subtract_compare_fusion.1) | copy-start | bytes 196
  79.9 116.2 %copy-start.38 = (f32[8,8]{0,1:T(8,128)}, f32[8,8]{0,1:T(8,128)S(1)}, u32[]{:S(2)}) copy-start(f32[8,8]{0,1:T(8,128)S(1)} %subtract_maximum_fusion.1) | copy-start | bytes 772
  80.0 113.3 %copy-start.40 = (f32[256,4]{0,1:T(4,128)}, f32[256,4]{0,1:T(4,128)S(1)}, u32[]{:S(2)}) copy-start(f32[256,4]{0,1:T(4,128)S(1)} %get-tuple-element.63) | copy-start | bytes 12292
  80.0 119.2 %copy-start.36 = (f32[256,4]{0,1:T(4,128)}, f32[256,4]{0,1:T(4,128)S(1)}, u32[]{:S(2)}) copy-start(f32[256,4]{0,1:T(4,128)S(1)} %get-tuple-element.64) | copy-start | bytes 12292
  80.5 107.0 %copy-start.15 = (f32[4,256,256]{2,1,0:T(8,128)}, f32[4,256,256]{2,1,0:T(8,128)S(1)}, u32[]{:S(2)}) copy-start(f32[4,256,256]{2,1,0:T(8,128)S(1)} %exponential_select_fusion) | copy-start | bytes 3145732
  212.9 11.9 copy-start.42
  234.3 223.0 %all-gather.7.cloned.1.call-start = ((), (), s32[]{:S(2)}) async-start(), calls=%async_computation.17 | async-start | bytes 10485760 | tf_op jit(solution)/shard_map/all_gather | solution.py:71
  377.8 53.8 %all-to-all-start.2 = ((bf16[8,256,512]{2,1,0:T(8,128)(2,1)}), bf16[8,256,512]{2,1,0:T(8,128)(2,1)}, u32[]{:S(2)}, u32[]{:S(2)}) async-start(bf16[8,256,512]{2,1,0:T(8,128)(2,1)} %param.11), calls=%async_computation.4 | async-start | bytes 4194304 | tf_op jit(solution)/shard_map/all_to_all | solution.py:164
  383.6 118.3 %all-gather.9.cloned.1.call-start = ((), (), s32[]{:S(2)}) async-start(), calls=%async_computation.19 | async-start | bytes 10485760 | tf_op jit(solution)/shard_map/all_gather | solution.py:45
  384.9 56.3 %copy-start.29 = (f32[2048]{0:T(1024)}, f32[2048]{0:T(1024)S(1)}, u32[]{:S(2)}) copy-start(f32[2048]{0:T(1024)S(1)} %fusion.50) | copy-start | bytes 24580
  445.2 227.5 %reduce-scatter.14.cloned.1.call-start = ((), (), s32[]{:S(2)}) async-start(), calls=%async_computation.18 | async-start | bytes 20971520 | tf_op jit(solution)/shard_map/reduce_scatter | solution.py:41
  547.5 252.7 %reduce-scatter.16.cloned.1.call-start = ((), (), s32[]{:S(2)}) async-start(), calls=%async_computation.20 | async-start | bytes 20971520 | tf_op jit(solution)/shard_map/reduce_scatter | solution.py:41
  579.6 220.7 %copy-start.27 = (f32[2048,1]{0,1:T(1,128)S(1)}, f32[2048,1]{0,1:T(1,128)}, u32[]{:S(2)}) copy-start(f32[2048,1]{0,1:T(1,128)} %copy-done.26) | copy-start | bytes 24580
  579.6 220.7 %copy-start.30 = (f32[2048]{0:T(1024)S(1)}, f32[2048]{0:T(1024)}, u32[]{:S(2)}) copy-start(f32[2048]{0:T(1024)} %copy-done.29) | copy-start | bytes 24580
  579.6 302.4 %all-gather.11.cloned.1.call-start = ((), (), s32[]{:S(2)}) async-start(), calls=%async_computation.21 | async-start | bytes 10485760 | tf_op jit(solution)/shard_map/all_gather | solution.py:45
  815.3 66.7 %copy-start.43 = (f32[2048,1]{0,1:T(1,128)S(1)}, f32[2048,1]{0,1:T(1,128)}, u32[]{:S(2)}) copy-start(f32[2048,1]{0,1:T(1,128)} %copy-done.42) | copy-start | bytes 24580
  822.9 321.6 %reduce-scatter.18.cloned.1.call-start = ((), (), s32[]{:S(2)}) async-start(), calls=%async_computation.22 | async-start | bytes 20971520 | tf_op jit(solution)/shard_map/reduce_scatter | solution.py:41
  945.0 8.6 copy-start.22
  945.0 8.6 copy-start.5
  945.0 8.5 copy-start.14
  945.0 8.5 copy-start.18
  966.4 8.2 copy-start.24
  966.4 8.2 copy-start.10
  966.4 8.2 copy-start.13
  977.6 8.4 copy-start.25
  977.6 8.4 copy-start.20
  977.6 8.4 copy-start.21
  1009.7 296.7 %reduce-scatter.32.cloned.1.call-start = ((), (), s32[]{:S(2)}) async-start(), calls=%async_computation.29 | async-start | bytes 6488064 | tf_op jit(solution)/shard_map/reduce_scatter | solution.py:260
  1028.3 473.7 %reduce-scatter.30.cloned.1.call-start = ((), (), s32[]{:S(2)}) async-start(), calls=%async_computation.28 | async-start | bytes 12976128 | tf_op jit(solution)/shard_map/reduce_scatter | solution.py:257
  1062.0 10.4 copy-start.23
  1062.0 511.7 %reduce-scatter.28.cloned.1.call-start = ((), (), s32[]{:S(2)}) async-start(), calls=%async_computation.27 | async-start | bytes 2359296 | tf_op jit(solution)/shard_map/reduce_scatter | solution.py:254
  1072.3 572.2 %reduce-scatter.22.cloned.1.call-start = ((), (), s32[]{:S(2)}) async-start(), calls=%async_computation.24 | async-start | bytes 2359296 | tf_op jit(solution)/shard_map/reduce_scatter | solution.py:245
  1082.0 633.6 %reduce-scatter.20.cloned.1.call-start = ((), (), s32[]{:S(2)}) async-start(), calls=%async_computation.23 | async-start | bytes 2359296 | tf_op jit(solution)/shard_map/reduce_scatter | solution.py:242
  1092.1 10.1 copy-start.19
  1092.1 694.5 %reduce-scatter.24.cloned.1.call-start = ((), (), s32[]{:S(2)}) async-start(), calls=%async_computation.25 | async-start | bytes 2359296 | tf_op jit(solution)/shard_map/reduce_scatter | solution.py:248
  1128.6 90.9 %all-to-all-start.1 = ((bf16[8,2,65536]{2,1,0:T(2,128)(2,1)}), bf16[8,2,65536]{2,1,0:T(2,128)(2,1)S(1)}, u32[]{:S(2)}, u32[]{:S(2)}) async-start(bf16[8,2,65536]{2,1,0:T(2,128)(2,1)} %reshape.389), calls=%async_computation.3 | async-start | bytes 4194304 | tf_op jit(solution)/shard_map/all_to_all | solution.py:267
  1134.4 10.1 copy-start.33
  1134.4 722.8 %reduce-scatter.26.cloned.1.call-start = ((), (), s32[]{:S(2)}) async-start(), calls=%async_computation.26 | async-start | bytes 2359296 | tf_op jit(solution)/shard_map/reduce_scatter | solution.py:251
  1144.4 10.9 copy-start.28
  1144.5 10.9 copy-start.31
  1144.5 10.9 copy-start.35
  1191.4 35.3 %copy-start.52 = (s32[8]{0:T(128)S(1)}, s32[8]{0:T(128)}, u32[]{:S(2)}) copy-start(s32[8]{0:T(128)} %param.12) | copy-start | bytes 100
  1219.5 639.5 %all-to-all-start.3 = ((bf16[8,2,65536]{2,1,0:T(2,128)(2,1)}), bf16[8,2,65536]{2,1,0:T(2,128)(2,1)}, u32[]{:S(2)}, u32[]{:S(2)}) async-start(bf16[8,2,65536]{2,1,0:T(2,128)(2,1)} %reshape.391), calls=%async_computation.7 | async-start | bytes 4194304 | tf_op jit(solution)/shard_map/all_to_all | solution.py:268
  1859.0 11.0 copy-start.1
  (25 other events, 88.6 us)
Sparse Core Ops, SparseCore 0:
  79.8 57.5 all-gather.4
  234.4 126.0 reduce-scatter.11
  377.9 58.8 all-gather.6
  445.4 56.4 all-gather.8
  547.7 125.0 reduce-scatter.13
  675.2 125.0 reduce-scatter.15
  823.0 58.8 all-gather.10
  1009.8 126.0 reduce-scatter.17
  1139.6 166.7 reduce-scatter.31
  1309.9 192.1 reduce-scatter.29
  1505.6 68.0 reduce-scatter.27
  1577.0 67.4 reduce-scatter.21
  1648.1 67.5 reduce-scatter.19
  1719.0 67.5 reduce-scatter.23
  1790.0 67.1 reduce-scatter.25
where the time goes:
time: 1880 us
  waiting for transfers between devices  1110 us (59%)
  matrix products  361 us (19%)
  blocking collectives  131 us (7%)
  local copies, waits for them, and re-layouts  129 us (7%)
  other arithmetic  113 us (6%)
  starting transfers between devices  19.7 us (1%)
    reduce_scatter x3, waiting for transfers between devices, to_shards(): lax.psum_scatter(partial_value, 'tensor', scatter_dimension=1, tiled=True)  221 us
    reduce_scatter x1, waiting for transfers between devices, local(): lax.psum_scatter(glu_term.astype(jnp.bfloat16), 'dp', scatter_dimension=0...  191 us
    reduce_scatter x1, waiting for transfers between devices, output_branch(): lax.psum_scatter(jnp.dot(gated_out, w_out, preferred_element_type=FLOAT),...  126 us
    dot_general x7, matrix products, contract_cols(): lax.dot_general(left, right, (((1,), (1,)), ((), ())), preferred_element_...  116 us
    dot_general x7, matrix products, contract_rows(): lax.dot_general(left, right, (((0,), (0,)), ((), ())), preferred_element_...  102 us
    reduce_scatter x1, waiting for transfers between devices, local(): lax.psum_scatter(down_term.astype(jnp.bfloat16), 'dp', scatter_dimension=...  78.4 us
    dot_general x5, matrix products, project(): jnp.dot(gathered, matrix, preferred_element_type=FLOAT)  77.5 us
    all_gather x2, waiting for transfers between devices, full_rows(): return lax.all_gather(values, 'tensor', axis=1, tiled=True)  71.3 us
  transfers between devices with their start and end apart: 18, of which 15 were waited for; matrix products, arithmetic and copies ran while one was open for 16% of the time, Pallas kernels for 0%

commit v1 on v0

v1 whole, which is shorter than its diff:
```python
import functools

import jax
import jax.numpy as jnp
from jax import lax
from jax.experimental import pallas as pl
from jax.experimental.pallas import tpu as pltpu
from jax.sharding import PartitionSpec as P

HEAD_DIM = 128
EPSILON = 1e-06
NARROW = jnp.bfloat16
FLOAT = jnp.float32
CHUNKS = 2

NN = (((1,), (0,)), ((), ()))
NT = (((1,), (1,)), ((), ()))
TN = (((0,), (0,)), ((), ()))


def mm(left, right, dims=NN):
    return lax.dot_general(left, right, dims, preferred_element_type=FLOAT)


def swap(value, axis, mask):
    size = lax.axis_size(axis)
    return lax.ppermute(value, axis, [(i, i ^ mask) for i in range(size)])


def gather_shards(value):
    size = lax.axis_size("tensor")
    shards = {0: value}
    mask = size // 2
    while mask:
        shards.update({k | mask: swap(v, "tensor", mask) for k, v in list(shards.items())})
        mask //= 2
    return [shards[k] for k in range(size)]


def scatter_terms(pieces):
    size = lax.axis_size("tensor")
    current = {k: [v] for k, v in enumerate(pieces)}
    mask = 1
    while mask < size:
        sent = {k: v for k, v in current.items() if k & mask}
        kept = {k: v for k, v in current.items() if not k & mask}
        for k, terms in sent.items():
            total = terms[0]
            if len(terms) > 1:
                total = sum(v.astype(FLOAT) for v in terms).astype(NARROW)
            kept[k ^ mask] = kept[k ^ mask] + [swap(total, "tensor", mask)]
        current = kept
        mask *= 2
    return current[0]


def total_rows(value, axes=("tensor",)):
    for axis in axes:
        mask = 1
        while mask < lax.axis_size(axis):
            value = value + swap(value, axis, mask)
            mask *= 2
    return value


def block_order(size):
    order = [0]
    while len(order) < size:
        order = [2 * k for k in order] + [2 * k + 1 for k in order]
    return order


def reduce_blocks(kept, sent):
    size = lax.axis_size("dp")
    mask = 1
    while True:
        arrived = swap(sent, "dp", mask)
        total = kept.astype(FLOAT) + arrived.astype(FLOAT)
        mask *= 2
        if mask >= size:
            return total
        half = total.shape[0] // 2
        narrow = total.astype(NARROW)
        kept, sent = narrow[:half], narrow[half:]


def to_row(column):
    wide = jnp.broadcast_to(column, (column.shape[0], 128))
    return jnp.transpose(wide)[:8]


def to_column(row):
    tall = jnp.broadcast_to(row[0:1], (128, row.shape[1]))
    return jnp.transpose(tall)[:, :1]


class Tiles:
    def __init__(self, chunk, chunks, seqs, span, group, heads):
        self.chunk, self.span, self.group, self.heads = chunk, span, group, heads
        self.rows = seqs * span
        self.chunk_seqs = seqs // chunks
        self.chunk_rows = self.chunk_seqs * span
        self.tile = group * span
        self.steps = self.chunk_seqs // group

    def spec(self, kind, shape):
        off = self.chunk * self.steps
        if kind == "rows":
            start = off if shape[0] == self.rows and self.rows != self.chunk_rows else 0
            return pl.BlockSpec((self.tile, shape[1]), lambda i, s: (start + i, 0))
        if kind == "vec":
            start = off if shape[1] == self.rows and self.rows != self.chunk_rows else 0
            return pl.BlockSpec((8, self.tile), lambda i, s: (0, start + i))
        if kind == "state":
            return pl.BlockSpec((self.group,) + tuple(shape[1:]), lambda i, s: (i, 0, 0, 0))
        zero = (0,) * len(shape)
        if kind == "acc":
            return pl.BlockSpec(tuple(shape), lambda i, s: zero)
        return pl.BlockSpec(tuple(shape), lambda i, s: zero, pipeline_mode=pl.Buffered(1))

    def call(self, name, body, scalars, ins, outs, scratch=(), flops=0):
        arrays = [a for _, a in ins]
        in_specs = [self.spec(kind, a.shape) for kind, a in ins]
        aliases, carried = {}, 0
        for n, out in enumerate(outs):
            if out[3] is not None:
                aliases[1 + len(arrays)] = n
                arrays.append(out[3])
                in_specs.append(pl.BlockSpec(memory_space=pl.ANY))
                carried += 1
        count = len(ins)

        def kernel(scalar_ref, *refs):
            first = count + carried
            body(scalar_ref, refs[:count], refs[first : first + len(outs)], refs[first + len(outs) :])

        moved = sum(self.tile * self.steps * 2 * 512 for _ in arrays)
        return pl.pallas_call(
            kernel,
            name=name,
            out_shape=[jax.ShapeDtypeStruct(o[1], o[2]) for o in outs],
            grid_spec=pltpu.PrefetchScalarGridSpec(
                num_scalar_prefetch=1,
                grid=(self.steps,),
                in_specs=in_specs,
                out_specs=[self.spec(o[0], o[1]) for o in outs],
                scratch_shapes=list(scratch),
            ),
            input_output_aliases=aliases,
            compiler_params=pltpu.CompilerParams(vmem_limit_bytes=60 * 1024 * 1024),
            cost_estimate=pl.CostEstimate(flops=int(flops), bytes_accessed=int(moved), transcendentals=0),
        )(scalars, *arrays)


def lanes(start, width):
    return pl.ds(pl.multiple_of(start, 128), width)


def valid_column(scalar_ref, tiles, piece):
    seq = tiles.chunk * tiles.chunk_seqs + pl.program_id(0) * tiles.group + piece
    place = lax.broadcasted_iota(jnp.int32, (tiles.span, 1), 0) + scalar_ref[1] * tiles.span
    return (place < scalar_ref[2 + seq]).astype(FLOAT)


def silu_slope(values):
    part = jax.nn.sigmoid(values)
    return part * (1.0 + values * (1.0 - part))


def assemble(scalar_ref, shards, target, scale, width):
    for k, shard in enumerate(shards):
        rows = shard[...]
        if scale is not None:
            rows = (rows.astype(FLOAT) * scale).astype(NARROW)
        target[:, lanes((scalar_ref[0] ^ k) * width, width)] = rows


def split_blocks(scalar_ref, source, kept, sent, order):
    half = len(order) // 2
    width = source.shape[1] // len(order)
    for place, k in enumerate(order):
        target = kept if place < half else sent
        at = (place % half) * width
        target[:, at : at + width] = source[:, lanes((scalar_ref[1] ^ k) * width, width)]


def inverse_rms(shards):
    total = None
    for shard in shards:
        rows = shard[...].astype(FLOAT)
        part = jnp.sum(rows * rows, axis=1, keepdims=True)
        total = part if total is None else total + part
    width = shards[0].shape[1] * len(shards)
    return lax.rsqrt(total / width + EPSILON)


def project_body(tiles, order, scalar_ref, ins, outs, scratch):
    size = len(ins) - 7
    shards = ins[:size]
    w_query, w_key, w_value, w_gate, inside, finish, _ = ins[size:]
    kept, sent, query_pre, key_pre, gate_pre, query, key, value, near, update, inverse_row = outs
    (normed,) = scratch
    inverse = inverse_rms(shards)
    inverse_row[...] = to_row(inverse)
    assemble(scalar_ref, shards, normed, inverse, shards[0].shape[1])
    split_blocks(scalar_ref, normed, kept, sent, order)
    pre = mm(normed[...], w_query[...])
    query_pre[...] = pre
    query[...] = (pre * jax.nn.sigmoid(pre)).astype(NARROW)
    pre = mm(normed[...], w_key[...])
    key_pre[...] = pre
    key[...] = (pre * jax.nn.sigmoid(pre)).astype(NARROW)
    value[...] = mm(normed[...], w_value[...]).astype(NARROW)
    gate_pre[...] = mm(normed[...], w_gate[...])
    for piece in range(tiles.group):
        rows = slice(piece * tiles.span, (piece + 1) * tiles.span)
        for head in range(tiles.heads):
            cols = slice(head * HEAD_DIM, (head + 1) * HEAD_DIM)
            k_head, v_head = key[rows, cols], value[rows, cols]
            scores = (mm(query[rows, cols], k_head, NT) * inside[head]).astype(NARROW)
            near[rows, cols] = mm(scores, v_head)
            keyed = (k_head.astype(FLOAT) * finish[:, cols]).astype(NARROW)
            update[piece, head] = mm(keyed, v_head, TN).astype(NARROW)


def mix_body(tiles, scalar_ref, ins, outs, scratch):
    query, near, gate_pre, state, start, w_out = ins
    mixture, square_row, *pieces = outs
    width = near.shape[1]
    for piece in range(tiles.group):
        rows = slice(piece * tiles.span, (piece + 1) * tiles.span)
        for head in range(tiles.heads):
            cols = slice(head * HEAD_DIM, (head + 1) * HEAD_DIM)
            far = mm(query[rows, cols], state[piece, head])
            mixture[rows, cols] = near[rows, cols] + far * start[:, cols]
    mixed = mixture[...]
    square_row[...] = to_row(jnp.sum(mixed * mixed, axis=1, keepdims=True))
    gated = (mixed * gate_pre[...]).astype(NARROW)
    for k, target in enumerate(pieces):
        target[...] = mm(gated, w_out[:, lanes((scalar_ref[0] ^ k) * width, width)]).astype(NARROW)


def mean_inverse(row, full):
    return lax.rsqrt(to_column(row[...]) / full + EPSILON)


def residual_body(tiles, full, scalar_ref, ins, outs, scratch):
    tokens, square_row, *terms = ins
    residual, narrow, attn, sums = outs

    @pl.when(pl.program_id(0) == 0)
    def _():
        sums[...] = jnp.zeros_like(sums)

    total = sum(term[...].astype(FLOAT) for term in terms)
    branch = total * mean_inverse(square_row, full)
    attn[...] = branch
    joined = tokens[...].astype(FLOAT) + branch
    residual[...] = joined
    narrow[...] = joined.astype(NARROW)
    for piece in range(tiles.group):
        rows = slice(piece * tiles.span, (piece + 1) * tiles.span)
        valid = valid_column(scalar_ref, tiles, piece)
        sums[0:1, :] += jnp.sum(valid * joined[rows] * joined[rows], axis=0, keepdims=True)
        sums[1:2, :] += jnp.sum(valid * branch[rows] * branch[rows], axis=0, keepdims=True)


def glu_body(tiles, order, scalar_ref, ins, outs, scratch):
    size = (len(ins) - 3) // 2
    shards, cot_shards = ins[:size], ins[size : 2 * size]
    w_first, w_up, w_down = ins[2 * size :]
    kept, sent, cot_kept, cot_sent, hidden, grad_gate, grad_up, inverse_row, inner_row = outs[:9]
    glu_pieces, grad_pieces = outs[9 : 9 + size], outs[9 + size :]
    normed, cot = scratch
    width = shards[0].shape[1]
    inverse = inverse_rms(shards)
    inverse_row[...] = to_row(inverse)
    assemble(scalar_ref, shards, normed, inverse, width)
    split_blocks(scalar_ref, normed, kept, sent, order)
    valid = jnp.concatenate([valid_column(scalar_ref, tiles, piece) for piece in range(tiles.group)], axis=0)
    assemble(scalar_ref, cot_shards, cot, valid, width)
    split_blocks(scalar_ref, cot, cot_kept, cot_sent, order)
    gate_half = mm(normed[...], w_first[...])
    up_half = mm(normed[...], w_up[...])
    product = gate_half * up_half
    hidden[...] = product.astype(NARROW)
    grad_hidden = mm(cot[...], w_down[...], NT)
    inner_row[...] = to_row(2.0 * jnp.sum(grad_hidden * product, axis=1, keepdims=True))
    grad_gate[...] = (grad_hidden * up_half).astype(NARROW)
    grad_up[...] = (grad_hidden * gate_half).astype(NARROW)
    for k in range(size):
        own = lanes((scalar_ref[0] ^ k) * width, width)
        grad_pieces[k][...] = (
            mm(grad_gate[...], w_first[own, :], NT) + mm(grad_up[...], w_up[own, :], NT)
        ).astype(NARROW)
    for k in range(size):
        own = lanes((scalar_ref[0] ^ k) * width, width)
        glu_pieces[k][...] = mm(hidden[...], w_down[:, own]).astype(NARROW)


def grad_residual_body(tiles, full, scalar_ref, ins, outs, scratch):
    cot, residual, attn, inverse_row, inner_row, *terms = ins
    grad_residual, narrow, inner_mix_row = outs
    total = sum(term[...].astype(FLOAT) for term in terms)
    inverse = to_column(inverse_row[...])
    inner = to_column(inner_row[...])
    valid = jnp.concatenate([valid_column(scalar_ref, tiles, piece) for piece in range(tiles.group)], axis=0)
    normed = residual[...] * inverse
    grad = valid * cot[...].astype(FLOAT) + inverse * (total - normed * (inner / full))
    grad_residual[...] = grad
    rounded = grad.astype(NARROW)
    narrow[...] = rounded
    inner_mix_row[...] = to_row(jnp.sum(rounded.astype(FLOAT) * attn[...], axis=1, keepdims=True))


def grad_mix_body(tiles, full, order, scalar_ref, ins, outs, scratch):
    size = len(ins) - 13
    shards = ins[:size]
    (mixture, gate_pre, query_pre, query, key, value, state, square_row, inner_row, inside, start, w_out, _) = ins[size:]
    kept, sent, gated, grad_gate_pre, grad_query_pre, grad_mix, grad_state, inner_one_row = outs
    whole, grad_query = scratch
    assemble(scalar_ref, shards, whole, None, shards[0].shape[1])
    split_blocks(scalar_ref, whole, kept, sent, order)
    grad_gated = mm(whole[...], w_out[...], NT)
    inverse = mean_inverse(square_row, full)
    inner = to_column(inner_row[...])
    gate = gate_pre[...]
    normed = mixture[...] * inverse
    gated[...] = (normed * gate).astype(NARROW)
    grad_gate = (grad_gated * normed).astype(NARROW)
    grad_gate_pre[...] = grad_gate
    grad_mix[...] = (inverse * (grad_gated * gate - normed * (inner / full))).astype(NARROW)
    for piece in range(tiles.group):
        rows = slice(piece * tiles.span, (piece + 1) * tiles.span)
        for head in range(tiles.heads):
            cols = slice(head * HEAD_DIM, (head + 1) * HEAD_DIM)
            grad_head = grad_mix[rows, cols]
            grad_scores = (mm(grad_head, value[rows, cols], NT) * inside[head]).astype(NARROW)
            grad_far = (grad_head.astype(FLOAT) * start[:, cols]).astype(NARROW)
            grad_query[rows, cols] = mm(grad_scores, key[rows, cols]) + mm(grad_far, state[piece, head], NT)
            grad_state[piece, head] = mm(query[rows, cols], grad_far, TN).astype(NARROW)
    pre = query_pre[...]
    grad_pre = (grad_query[...] * silu_slope(pre)).astype(NARROW)
    grad_query_pre[...] = grad_pre
    inner_one_row[...] = to_row(
        jnp.sum(grad_pre.astype(FLOAT) * pre + grad_gate.astype(FLOAT) * gate, axis=1, keepdims=True)
    )


def grad_key_body(tiles, scalar_ref, ins, outs, scratch):
    (query, key, value, grad_mix, grad_update, key_pre, grad_query_pre, grad_gate_pre, inner_in) = ins[:9]
    inside, finish, w_query, w_key, w_value, w_gate = ins[9:]
    grad_key_pre, grad_value_pre, inner_row, *pieces = outs
    (grad_key,) = scratch
    width = key.shape[1]
    for piece in range(tiles.group):
        rows = slice(piece * tiles.span, (piece + 1) * tiles.span)
        for head in range(tiles.heads):
            cols = slice(head * HEAD_DIM, (head + 1) * HEAD_DIM)
            q_head, k_head, v_head = query[rows, cols], key[rows, cols], value[rows, cols]
            grad_head, grad_up = grad_mix[rows, cols], grad_update[piece, head]
            scores = (mm(q_head, k_head, NT) * inside[head]).astype(NARROW)
            grad_scores = (mm(grad_head, v_head, NT) * inside[head]).astype(NARROW)
            keyed = (k_head.astype(FLOAT) * finish[:, cols]).astype(NARROW)
            grad_key[rows, cols] = mm(grad_scores, q_head, TN) + mm(v_head, grad_up, NT) * finish[:, cols]
            grad_value_pre[rows, cols] = (mm(scores, grad_head, TN) + mm(keyed, grad_up)).astype(NARROW)
    pre = key_pre[...]
    grad_pre = (grad_key[...] * silu_slope(pre)).astype(NARROW)
    grad_key_pre[...] = grad_pre
    grad_value = grad_value_pre[...]
    inner = jnp.sum(
        grad_pre.astype(FLOAT) * pre + grad_value.astype(FLOAT) * value[...].astype(FLOAT), axis=1, keepdims=True
    )
    inner_row[...] = inner_in[...] + to_row(inner)
    for k, target in enumerate(pieces):
        own = lanes((scalar_ref[0] ^ k) * width, width)
        target[...] = (
            mm(grad_query_pre[...], w_query[own, :], NT)
            + mm(grad_pre, w_key[own, :], NT)
            + mm(grad_value, w_value[own, :], NT)
            + mm(grad_gate_pre[...], w_gate[own, :], NT)
        ).astype(NARROW)


def input_grad_body(tiles, full, scalar_ref, ins, outs, scratch):
    tokens, grad_residual, inverse_row, inner_row, *terms = ins
    (target,) = outs
    total = sum(term[...].astype(FLOAT) for term in terms)
    inverse = to_column(inverse_row[...])
    inner = to_column(inner_row[...])
    normed = tokens[...].astype(FLOAT) * inverse
    target[...] = (grad_residual[...] + inverse * (total - normed * (inner / full))).astype(NARROW)


def output_body(tiles, scalar_ref, ins, outs, scratch):
    residual, *terms = ins
    target, sums = outs

    @pl.when(pl.program_id(0) == 0)
    def _():
        sums[...] = jnp.zeros_like(sums)

    total = sum(term[...].astype(FLOAT) for term in terms)
    joined = residual[...] + total
    for piece in range(tiles.group):
        rows = slice(piece * tiles.span, (piece + 1) * tiles.span)
        valid = valid_column(scalar_ref, tiles, piece)
        target[rows, :] = (valid * joined[rows]).astype(NARROW)
        sums[0:1, :] += jnp.sum(valid * total[rows] * total[rows], axis=0, keepdims=True)


def scan_body(reverse, source, decay, target):
    count = source.shape[0]
    carried = jnp.zeros(source.shape[1:], FLOAT)
    for block in reversed(range(count)) if reverse else range(count):
        target[block] = carried.astype(NARROW)
        carried = decay[...] * carried + source[block].astype(FLOAT)


def share_states(update, slopes, span, reverse):
    size = lax.axis_size("dp")
    seqs, heads = update.shape[:2]
    parts = size // seqs
    group = heads // parts
    own = lax.dynamic_slice_in_dim(slopes, (lax.axis_index("dp") % parts) * group, group)
    decay = jnp.broadcast_to(jnp.exp(-own * span)[:, None, None], (group, HEAD_DIM, HEAD_DIM))
    blocks = update.reshape(size, group, HEAD_DIM, HEAD_DIM)
    arrived = lax.all_to_all(blocks, "dp", 0, 0, tiled=True)
    summed = pl.pallas_call(
        functools.partial(scan_body, reverse),
        name="scan_states",
        out_shape=jax.ShapeDtypeStruct(arrived.shape, NARROW),
    )(arrived, decay)
    returned = lax.all_to_all(summed, "dp", 0, 0, tiled=True)
    return returned.reshape(update.shape)


def local(tokens, cotangent, lengths, w_query, w_key, w_value, w_gate, w_out, w_glu_in, w_glu_out):
    seqs, span, width = tokens.shape
    dp_size, tensor_size = lax.axis_size("dp"), lax.axis_size("tensor")
    rows, full = seqs * span, width * tensor_size
    ff = w_glu_out.shape[0]
    heads = width // HEAD_DIM
    tensor_index, dp_index = lax.axis_index("tensor"), lax.axis_index("dp")
    scalars = jnp.concatenate([jnp.stack([tensor_index, dp_index]).astype(jnp.int32), lengths])
    order = block_order(dp_size)
    chunks = CHUNKS
    group = max(1, 256 // span)
    wide = seqs // chunks
    half_full = full // 2

    head_ids = (tensor_index * heads + jnp.arange(heads, dtype=jnp.int32)).astype(FLOAT)
    slopes = jnp.exp2(-8.0 * (head_ids + 1.0) / (heads * tensor_size))
    places = jnp.arange(span).astype(FLOAT)
    distance = places[:, None] - places[None, :]
    inside = jnp.where(distance >= 0, jnp.exp(-slopes[:, None, None] * jnp.maximum(distance, 0.0)), 0.0)
    lane_slopes = jnp.repeat(slopes, HEAD_DIM)
    start = jnp.exp(-lane_slopes[None, :] * (places[:, None] + 1.0))
    finish = jnp.exp(-lane_slopes[None, :] * (span - 1.0 - places[:, None]))

    token_rows = tokens.reshape(rows, width)
    cot_rows = cotangent.reshape(rows, width)
    w_first, w_up = w_glu_in[:, 0, :], w_glu_in[:, 1, :]
    tiles = [Tiles(n, chunks, seqs, span, group, heads) for n in range(chunks)]
    broad = [Tiles(n, chunks, seqs, span, wide, heads) for n in range(chunks)]
    part_rows = rows // chunks

    def cut(array, n):
        return array[n * part_rows : (n + 1) * part_rows]

    def full_outs(shapes, carried):
        return [("rows", (rows, s), NARROW, None if carried is None else carried[n]) for n, s in enumerate(shapes)]

    def part(size, dtype=FLOAT):
        return ("rows", (part_rows, size), dtype, None)

    vec = ("vec", (8, part_rows), FLOAT, None)
    pieces = [part(width, NARROW)] * tensor_size
    state_shape = ("state", (wide, heads, HEAD_DIM, HEAD_DIM), NARROW, None)

    x_shards = [gather_shards(cut(token_rows, n)) for n in range(chunks)]
    cot_shards = [gather_shards(cut(cot_rows, n)) for n in range(chunks)]
    saved = [{} for _ in range(chunks)]
    carried_one = carried_two = carried_three = carried_four = None
    sums_a = jnp.zeros((2,), FLOAT)
    for n in range(chunks):
        s = saved[n]
        out = tiles[n].call(
            "project",
            functools.partial(project_body, tiles[n], order),
            scalars,
            [("rows", v) for v in x_shards[n]]
            + [("whole", v) for v in (w_query, w_key, w_value, w_gate, inside, finish, start)],
            full_outs([half_full] * 2, carried_one)
            + [part(width)] * 3
            + [part(width, NARROW)] * 3
            + [part(width), state_shape, vec],
            [pltpu.VMEM((tiles[n].tile, full), NARROW)],
            flops=2 * part_rows * full * width * 4,
        )
        carried_one = out[:2]
        s["qz"], s["kz"], s["uz"], s["q"], s["k"], s["v"], near, update, s["inv1"] = out[2:]
        s["state"] = share_states(update, slopes, span, False)
        out = tiles[n].call(
            "mix",
            functools.partial(mix_body, tiles[n]),
            scalars,
            [("rows", s["q"]), ("rows", near), ("rows", s["uz"]), ("state", s["state"]), ("whole", start), ("whole", w_out)],
            [part(width), vec] + pieces,
            flops=2 * part_rows * full * width,
        )
        s["mix"], square = out[:2]
        s["square"] = total_rows(square)
        terms = scatter_terms(out[2:])
        s["residual"], s["narrow"], s["attn"], sums = broad[n].call(
            "residual",
            functools.partial(residual_body, broad[n], full),
            scalars,
            [("rows", token_rows), ("vec", s["square"])] + [("rows", v) for v in terms],
            [part(width), part(width, NARROW), part(width), ("acc", (8, width), FLOAT, None)],
        )
        sums_a = sums_a + jnp.sum(sums[:2], axis=1)
    sums_b = jnp.zeros((), FLOAT)
    for n in range(chunks):
        s = saved[n]
        shards = gather_shards(s["narrow"])
        out = tiles[n].call(
            "glu",
            functools.partial(glu_body, tiles[n], order),
            scalars,
            [("rows", v) for v in shards + cot_shards[n]] + [("whole", v) for v in (w_first, w_up, w_glu_out)],
            full_outs([half_full] * 4 + [ff] * 3, carried_two) + [vec, vec] + pieces + pieces,
            [pltpu.VMEM((tiles[n].tile, full), NARROW)] * 2,
            flops=2 * part_rows * full * ff * 6,
        )
        carried_two = out[:7]
        s["inv2"], inner = out[7:9]
        s["glu"] = out[9 : 9 + tensor_size]
        terms = scatter_terms(out[9 + tensor_size :])
        s["grad_residual"], s["grad_narrow"], s["inner_mix"] = broad[n].call(
            "grad_residual",
            functools.partial(grad_residual_body, broad[n], full),
            scalars,
            [("rows", cot_rows), ("rows", s["residual"]), ("rows", s["attn"]), ("vec", s["inv2"]), ("vec", total_rows(inner))]
            + [("rows", v) for v in terms],
            [part(width), part(width, NARROW), vec],
        )
    two_kept, two_sent, cot_kept, cot_sent, hidden, grad_gate, grad_up = carried_two

    def weight_term(kept, sent, right):
        return reduce_blocks(
            mm(kept, right, TN).astype(NARROW),
            mm(sent, right, TN).astype(NARROW),
        )

    down_part = weight_term(cot_kept, cot_sent, hidden)
    first_part = weight_term(two_kept, two_sent, grad_gate)
    up_part = weight_term(two_kept, two_sent, grad_up)
    for n in range(chunks):
        s = saved[n]
        shards = gather_shards(s["grad_narrow"])
        inner_mix = total_rows(s["inner_mix"])
        out = tiles[n].call(
            "grad_mix",
            functools.partial(grad_mix_body, tiles[n], full, order),
            scalars,
            [("rows", v) for v in shards]
            + [("rows", s[key]) for key in ("mix", "uz", "qz", "q", "k", "v")]
            + [("state", s["state"]), ("vec", s["square"]), ("vec", inner_mix)]
            + [("whole", v) for v in (inside, start, w_out, finish)],
            full_outs([half_full] * 2 + [width] * 3, carried_three) + [part(width, NARROW), state_shape, vec],
            [pltpu.VMEM((tiles[n].tile, full), NARROW), pltpu.VMEM((tiles[n].tile, width), FLOAT)],
            flops=2 * part_rows * full * width,
        )
        carried_three = out[:5]
        grad_mix, grad_state, inner_one = out[5:]
        grad_update = share_states(grad_state, slopes, span, True)
        out = tiles[n].call(
            "grad_key",
            functools.partial(grad_key_body, tiles[n]),
            scalars,
            [("rows", s["q"]), ("rows", s["k"]), ("rows", s["v"]), ("rows", grad_mix), ("state", grad_update)]
            + [("rows", s["kz"]), ("rows", carried_three[4]), ("rows", carried_three[3]), ("vec", inner_one)]
            + [("whole", v) for v in (inside, finish, w_query, w_key, w_value, w_gate)],
            full_outs([width] * 2, carried_four) + [vec] + pieces,
            [pltpu.VMEM((tiles[n].tile, width), FLOAT)],
            flops=2 * part_rows * full * width * 4,
        )
        carried_four = out[:2]
        s["inner_one"] = out[2]
        s["grad_pieces"] = out[3:]
    out_kept, out_sent, gated, grad_gate_pre, grad_query_pre = carried_three
    out_part = weight_term(out_kept, out_sent, gated)
    one_kept, one_sent = carried_one
    gate_part = weight_term(one_kept, one_sent, grad_gate_pre)
    query_part = weight_term(one_kept, one_sent, grad_query_pre)
    key_part = weight_term(one_kept, one_sent, carried_four[0])
    value_part = weight_term(one_kept, one_sent, carried_four[1])
    output = input_grad = None
    for n in range(chunks):
        s = saved[n]
        output, sums = broad[n].call(
            "output",
            functools.partial(output_body, broad[n]),
            scalars,
            [("rows", s["residual"])] + [("rows", v) for v in scatter_terms(s["glu"])],
            [("rows", (rows, width), NARROW, output), ("acc", (8, width), FLOAT, None)],
        )
        sums_b = sums_b + jnp.sum(sums[0])
        (input_grad,) = broad[n].call(
            "input_grad",
            functools.partial(input_grad_body, broad[n], full),
            scalars,
            [("rows", token_rows), ("rows", s["grad_residual"]), ("vec", s["inv1"]), ("vec", total_rows(s["inner_one"]))]
            + [("rows", v) for v in scatter_terms(s["grad_pieces"])],
            [("rows", (rows, width), NARROW, input_grad)],
        )
    totals = total_rows(jnp.concatenate([sums_a, sums_b[None]]), ("tensor", "dp"))
    token_count = jnp.sum(lengths).astype(FLOAT)
    rms_values = jnp.sqrt(totals / (token_count * full) + EPSILON)
    return (
        output.reshape(tokens.shape),
        input_grad.reshape(tokens.shape),
        query_part,
        key_part,
        value_part,
        gate_part,
        out_part.T,
        jnp.stack([first_part, up_part], axis=1),
        down_part.T,
        rms_values,
    )


def solution(mesh):
    in_specs = (
        P(None, "dp", "tensor"),
        P(None, "dp", "tensor"),
        P(),
        P(None, "tensor"),
        P(None, "tensor"),
        P(None, "tensor"),
        P(None, "tensor"),
        P("tensor", None),
        P(None, None, "tensor"),
        P("tensor", None),
    )
    out_specs = (
        P(None, "dp", "tensor"),
        P(None, "dp", "tensor"),
        P("dp", "tensor"),
        P("dp", "tensor"),
        P("dp", "tensor"),
        P("dp", "tensor"),
        P("tensor", "dp"),
        P("dp", None, "tensor"),
        P("tensor", "dp"),
        P(),
    )
    return jax.shard_map(local, mesh=mesh, in_specs=in_specs, out_specs=out_specs, check_vma=False)
```

time: 1880 us -> 1170 us (0.62)
  waiting for transfers between devices: 1110 us -> 552 us
  Pallas kernels: 0 us -> 297 us
  matrix products: 361 us -> 93.8 us
  blocking collectives: 131 us -> 0 us
  starting transfers between devices: 19.7 us -> 96.4 us
  local copies, waits for them, and re-layouts: 129 us -> 65.6 us
  other arithmetic: 113 us -> 51.2 us
    reduce_scatter x11 -> x0, waiting for transfers between devices: 911 us -> none  [the longest x3 221 us: to_shards(): lax.psum_scatter(partial_value, 'tensor', scatter_dimension=1, tiled=True)]
    ppermute x0 -> x93, waiting for transfers between devices: none -> 494 us  [swap(): return lax.ppermute(value, axis, [(i, i ^ mask) for i in range(size)])]
    pallas_call x0 -> x22, Pallas kernels: none -> 297 us  [the longest x18 289 us: call(): pl.pallas_call(kernel, name=name, out_shape=[jax.ShapeDtypeStruct(o[1], o...]
    dot_general x35 -> x16, matrix products: 361 us -> 93.8 us  [mm(): return lax.dot_general(left, right, dims, preferred_element_type=FLOAT)]
    all_gather x4 -> x0, waiting for transfers between devices: 128 us -> none  [the longest x2 71.3 us: full_rows(): return lax.all_gather(values, 'tensor', axis=1, tiled=True)]
    psum x7 -> x0, blocking collectives: 75.6 us -> none  [the longest x1 39.8 us: local(): totals = lax.psum(local_sums, ('dp', 'tensor'))]
    ppermute x0 -> x93, starting transfers between devices: none -> 61 us  [swap(): return lax.ppermute(value, axis, [(i, i ^ mask) for i in range(size)])]
    all_to_all x1 -> x0, blocking collectives: 55.8 us -> none  [local(): lax.all_to_all(tokens, 'dp', split_axis=0, concat_axis=1, tiled=True)]
  transfers between devices with their start and end apart: 18 -> 101, of which waited for: 15 -> 35; matrix products, arithmetic and copies ran while one was open for 16% -> 17% of each run, Pallas kernels for 0% -> 24%
where the time goes in v1:
time: 1170 us; the launch traced here: 1160 us
  waiting for transfers between devices  552 us (47%)
  Pallas kernels  297 us (25%)
  starting transfers between devices  96.4 us (8%)
  matrix products  93.8 us (8%)
  local copies, waits for them, and re-layouts  65.6 us (6%)
  other arithmetic  51.2 us (4%)
    ppermute x93, waiting for transfers between devices, swap(): return lax.ppermute(value, axis, [(i, i ^ mask) for i in range(size)])  494 us
    pallas_call x18, Pallas kernels, call(): pl.pallas_call(kernel, name=name, out_shape=[jax.ShapeDtypeStruct(o[1], o...  289 us
    dot_general x16, matrix products, mm(): return lax.dot_general(left, right, dims, preferred_element_type=FLOAT)  93.8 us
    ppermute x93, starting transfers between devices, swap(): return lax.ppermute(value, axis, [(i, i ^ mask) for i in range(size)])  61 us
    all_to_all x4, waiting for transfers between devices, share_states(): arrived = lax.all_to_all(blocks, 'dp', 0, 0, tiled=True)  38.7 us
  transfers between devices with their start and end apart: 101, of which 35 were waited for; matrix products, arithmetic and copies ran while one was open for 17% of the time, Pallas kernels for 24%

profile of v1, /device:TPU:0, one launch (start us, length us, event | category | flops | bytes accessed | tf_op | source)
XLA Modules:
  0.0 1159.5 jit_solution(8066149798796498316)
XLA Ops:
  6.1 23.5 %collective-permute-done.4.refs_2_ = bf16[1024,512]{1,0:T(8,128)(2,1)} collective-permute-done((bf16[1024,512]{1,0:T(8,128)(2,1)S(1)}, bf16[1024,512]{1,0:T(8,128)(2,1)}, u32[]{:S(2)}, u32[]{:S(2)}) %collective-permute-start.4) | collective-permute-done | bytes 1048608 | tf_op jit(solution)/shard_map/ppermute | solution.py:27
  31.0 20.2 %collective-permute-done.1.refs_2_ = bf16[1024,512]{1,0:T(8,128)(2,1)} collective-permute-done((bf16[1024,512]{1,0:T(8,128)(2,1)S(1)}, bf16[1024,512]{1,0:T(8,128)(2,1)}, u32[]{:S(2)}, u32[]{:S(2)}) %collective-permute-start.1) | collective-permute-done | bytes 1048608 | tf_op jit(solution)/shard_map/ppermute | solution.py:27
  53.1 21.6 %project.2 = (bf16[2048,1024]{1,0:T(8,128)(2,1)}, bf16[2048,1024]{1,0:T(8,128)(2,1)}, f32[1024,512]{1,0:T(8,128)}, f32[1024,512]{1,0:T(8,128)}, f32[1024,512]{1,...) custom-call(s32[10]{0:T(128)} %pad_add_fusion.scalar_ref, ...), custom_call_target="tpu_custom_call" | custom-call | flops 8589934592 | bytes 11534336 | tf_op jit(solution)/shard_map/project/pallas_call | solution.py:138
  74.7 6.0 all-to-all-start.2
  80.7 21.0 %project.3 = (bf16[2048,1024]{1,0:T(8,128)(2,1)}, bf16[2048,1024]{1,0:T(8,128)(2,1)}, f32[1024,512]{1,0:T(8,128)}, f32[1024,512]{1,0:T(8,128)}, f32[1024,512]{1,...) custom-call(s32[10]{0:T(128)} %pad_add_fusion.scalar_ref, ...), custom_call_target="tpu_custom_call", output_to_operand_aliasing={{0}: (12, {}), {1}: (13, {})} | custom-call | flops 8589934592 | bytes 13631488 | tf_op jit(solution)/shard_map/project/pallas_call | solution.py:138
  110.5 11.8 %all-to-all-done.source = bf16[8,2,128,128]{3,2,1,0:T(8,128)(2,1)S(1)} async-done(((bf16[8,2,128,128]{3,2,1,0:T(8,128)(2,1)}), bf16[8,2,128,128]{3,2,1,0:T(8,128)(2,1)S(1)}, u32[]{:S(2)}, u32[]{:S(2)}) %all-to-all-start) | async-done | bytes 524320 | tf_op jit(solution)/shard_map/all_to_all | solution.py:428
  127.9 12.7 %all-to-all-done.3 = bf16[8,2,128,128]{3,2,1,0:T(8,128)(2,1)S(1)} async-done(((bf16[8,2,128,128]{3,2,1,0:T(8,128)(2,1)}), bf16[8,2,128,128]{3,2,1,0:T(8,128)(2,1)S(1)}, u32[]{:S(2)}, u32[]{:S(2)}) %all-to-all-start.3) | async-done | bytes 524320 | tf_op jit(solution)/shard_map/all_to_all | solution.py:434
  144.5 8.7 mix.3
  159.9 8.8 mix.2
  175.5 20.8 %collective-permute-done.18 = f32[8,1024]{1,0:T(8,128)S(1)} collective-permute-done((f32[8,1024]{1,0:T(8,128)S(1)}, f32[8,1024]{1,0:T(8,128)S(1)}, u32[]{:S(2)}, u32[]{:S(2)}) %collective-permute-start.18) | collective-permute-done | bytes 32800 | tf_op jit(solution)/shard_map/ppermute | solution.py:27
  200.1 6.4 residual.3
  206.5 13.0 %collective-permute-done.7 = f32[8,1024]{1,0:T(8,128)S(1)} collective-permute-done((f32[8,1024]{1,0:T(8,128)S(1)}, f32[8,1024]{1,0:T(8,128)S(1)}, u32[]{:S(2)}, u32[]{:S(2)}) %collective-permute-start.7) | collective-permute-done | bytes 32800 | tf_op jit(solution)/shard_map/ppermute | solution.py:27
  221.0 22.8 %fusion.3 = (bf16[2048,1,1408]{2,1,0:T(2,128)(2,1)}, bf16[2048,1,1408]{2,1,0:T(2,128)(2,1)}) fusion(bf16[2048,2,1408]{2,1,0:T(2,128)(2,1)} %param.18), kind=kLoop, calls=%fused_computation.70 | loop fusion | bytes 23068672 | tf_op jit(solution)/shard_map/slice | solution.py:463
  245.5 6.6 residual.2
  253.5 11.0 collective-permute-done.23.refs_2_
  264.6 16.9 %copy_bitcast_fusion = (bf16[2048,1408]{1,0:T(8,128)(2,1)}, bf16[2048,1408]{1,0:T(8,128)(2,1)}) fusion(bf16[2048,1,1408]{2,1,0:T(2,128)(2,1)} %get-tuple-element.252, bf16[2048,1,1408]{2,1,0:T(2,128)(2,1)} %get-tuple-element.253), kind=kLoop, calls=%fused_computation | loop fusion | bytes 23068672 | tf_op jit(solution)/shard_map/squeeze | solution.py:463
  287.6 21.0 %collective-permute-done.12.refs_2_ = bf16[1024,512]{1,0:T(8,128)(2,1)} collective-permute-done((bf16[1024,512]{1,0:T(8,128)(2,1)}, bf16[1024,512]{1,0:T(8,128)(2,1)}, u32[]{:S(2)}, u32[]{:S(2)}) %collective-permute-start.12) | collective-permute-done | bytes 1048608 | tf_op jit(solution)/shard_map/ppermute | solution.py:27
  308.6 54.1 %glu.2 = (bf16[2048,1024]{1,0:T(8,128)(2,1)}, bf16[2048,1024]{1,0:T(8,128)(2,1)}, bf16[2048,1024]{1,0:T(8,128)(2,1)}, bf16[2048,1024]{1,0:T(8,128)(2,1)}, bf16[2...) custom-call(s32[10]{0:T(128)} %pad_add_fusion.scalar_ref, ...), custom_call_target="tpu_custom_call" | custom-call | flops 35433480192 | bytes 11534336 | tf_op jit(solution)/shard_map/glu/pallas_call | solution.py:138
  363.4 54.5 %glu.3 = (bf16[2048,1024]{1,0:T(8,128)(2,1)}, bf16[2048,1024]{1,0:T(8,128)(2,1)}, bf16[2048,1024]{1,0:T(8,128)(2,1)}, bf16[2048,1024]{1,0:T(8,128)(2,1)}, bf16[2...) custom-call(s32[10]{0:T(128)} %pad_add_fusion.scalar_ref, ...), custom_call_target="tpu_custom_call", output_to_operand_aliasing={{0}: (12, {}), {1}: (13, {}), {2}: (14, {}), {3}: (15, {}),... | custom-call | flops 35433480192 | bytes 18874368 | tf_op jit(solution)/shard_map/glu/pallas_call | solution.py:138
  418.4 11.5 convolution_convert_fusion.5
  429.9 8.3 convolution_convert_fusion.4
  438.8 8.2 convolution_convert_fusion.3
  454.1 8.1 convolution_convert_fusion
  466.3 32.9 %collective-permute-done.45 = f32[8,1024]{1,0:T(8,128)S(1)} collective-permute-done((f32[8,1024]{1,0:T(8,128)S(1)}, f32[8,1024]{1,0:T(8,128)S(1)}, u32[]{:S(2)}, u32[]{:S(2)}) %collective-permute-start.45) | collective-permute-done | bytes 32800 | tf_op jit(solution)/shard_map/ppermute | solution.py:27
  503.0 8.3 convolution_convert_fusion.2
  529.7 7.4 grad_residual.2
  537.2 11.7 %collective-permute-done.48.refs_7_ = bf16[1024,512]{1,0:T(8,128)(2,1)} collective-permute-done((bf16[1024,512]{1,0:T(8,128)(2,1)}, bf16[1024,512]{1,0:T(8,128)(2,1)}, u32[]{:S(2)}, u32[]{:S(2)}) %collective-permute-start.48) | collective-permute-done | bytes 1048608 | tf_op jit(solution)/shard_map/ppermute | solution.py:27
  548.9 7.4 grad_residual.3
  560.7 124.8 %collective-permute-done.90 = f32[3]{0:T(128)S(1)} collective-permute-done((f32[3]{0:T(128)S(1)}, f32[3]{0:T(128)S(1)}, u32[]{:S(2)}, u32[]{:S(2)}) %collective-permute-start.90) | collective-permute-done | bytes 44 | tf_op jit(solution)/shard_map/ppermute | solution.py:27
  690.6 10.6 convolution_convert_fusion.1
  732.6 9.3 collective-permute-done.40.refs_2_
  743.0 13.2 %grad_mix.2 = (bf16[2048,1024]{1,0:T(8,128)(2,1)}, bf16[2048,1024]{1,0:T(8,128)(2,1)}, bf16[2048,512]{1,0:T(8,128)(2,1)}, bf16[2048,512]{1,0:T(8,128)(2,1)}, bf1...) custom-call(s32[10]{0:T(128)} %pad_add_fusion.scalar_ref, ...), custom_call_target="tpu_custom_call" | custom-call | flops 2147483648 | bytes 17825792 | tf_op jit(solution)/shard_map/grad_mix/pallas_call | solution.py:138
  764.5 37.2 %collective-permute-done.80 = bf16[512,1408]{1,0:T(8,128)(2,1)} collective-permute-done((bf16[512,1408]{1,0:T(8,128)(2,1)}, bf16[512,1408]{1,0:T(8,128)(2,1)}, u32[]{:S(2)}, u32[]{:S(2)}) %collective-permute-start.80) | collective-permute-done | bytes 1441824 | tf_op jit(solution)/shard_map/ppermute | solution.py:27
  804.4 40.6 %collective-permute-done.83 = bf16[512,1408]{1,0:T(8,128)(2,1)} collective-permute-done((bf16[512,1408]{1,0:T(8,128)(2,1)}, bf16[512,1408]{1,0:T(8,128)(2,1)}, u32[]{:S(2)}, u32[]{:S(2)}) %collective-permute-start.83) | collective-permute-done | bytes 1441824 | tf_op jit(solution)/shard_map/ppermute | solution.py:27
  857.0 25.2 %collective-permute-done.81 = bf16[256,1408]{1,0:T(8,128)(2,1)} collective-permute-done((bf16[256,1408]{1,0:T(8,128)(2,1)}, bf16[256,1408]{1,0:T(8,128)(2,1)}, u32[]{:S(2)}, u32[]{:S(2)}) %collective-permute-start.81) | collective-permute-done | bytes 720928 | tf_op jit(solution)/shard_map/ppermute | solution.py:27
  887.6 9.9 collective-permute-done.84
  903.5 21.6 %grad_key.2 = (bf16[2048,512]{1,0:T(8,128)(2,1)}, bf16[2048,512]{1,0:T(8,128)(2,1)}, f32[8,1024]{1,0:T(8,128)}, bf16[1024,512]{1,0:T(8,128)(2,1)}, bf16[1024,512...) custom-call(s32[10]{0:T(128)} %pad_add_fusion.scalar_ref, ...), custom_call_target="tpu_custom_call" | custom-call | flops 8589934592 | bytes 15728640 | tf_op jit(solution)/shard_map/grad_key/pallas_call | solution.py:138
  925.2 13.7 %grad_mix.3 = (bf16[2048,1024]{1,0:T(8,128)(2,1)}, bf16[2048,1024]{1,0:T(8,128)(2,1)}, bf16[2048,512]{1,0:T(8,128)(2,1)}, bf16[2048,512]{1,0:T(8,128)(2,1)}, bf1...) custom-call(s32[10]{0:T(128)} %pad_add_fusion.scalar_ref, ...), custom_call_target="tpu_custom_call", output_to_operand_aliasing={{0}: (18, {}), {1}: (19, {}), {2}: (20, {}), {3}: (21, {}),... | custom-call | flops 2147483648 | bytes 23068672 | tf_op jit(solution)/shard_map/grad_mix/pallas_call | solution.py:138
  938.9 6.4 convolution_convert_fusion.6
  957.6 6.4 convolution_convert_fusion.15
  974.1 26.9 %all-to-all-done.4.source = bf16[8,2,128,128]{3,2,1,0:T(8,128)(2,1)S(1)} async-done(((bf16[8,2,128,128]{3,2,1,0:T(8,128)(2,1)}), bf16[8,2,128,128]{3,2,1,0:T(8,128)(2,1)S(1)}, u32[]{:S(2)}, u32[]{:S(2)}) %all-to-all-start.4) | async-done | bytes 524320 | tf_op jit(solution)/shard_map/all_to_all | solution.py:428
  1013.9 6.2 collective-permute-done.64
  1022.3 11.8 %collective-permute-done.77 = bf16[512,512]{1,0:T(8,128)(2,1)S(1)} collective-permute-done((bf16[512,512]{1,0:T(8,128)(2,1)S(1)}, bf16[512,512]{1,0:T(8,128)(2,1)S(1)}, u32[]{:S(2)}, u32[]{:S(2)}) %collective-permute-start.77) | collective-permute-done | bytes 524320 | tf_op jit(solution)/shard_map/ppermute | solution.py:27
  1042.5 7.1 collective-permute-done.65
  1049.9 21.6 %grad_key.3 = (bf16[2048,512]{1,0:T(8,128)(2,1)}, bf16[2048,512]{1,0:T(8,128)(2,1)}, f32[8,1024]{1,0:T(8,128)}, bf16[1024,512]{1,0:T(8,128)(2,1)}, bf16[1024,512...) custom-call(s32[10]{0:T(128)} %pad_add_fusion.scalar_ref, ...), custom_call_target="tpu_custom_call", output_to_operand_aliasing={{0}: (16, {}), {1}: (17, {})} | custom-call | flops 8589934592 | bytes 17825792 | tf_op jit(solution)/shard_map/grad_key/pallas_call | solution.py:138
  1090.2 10.2 collective-permute-done.70
  1100.8 10.9 collective-permute-done.67
  1129.4 12.4 %collective-permute-done.55 = f32[8,1024]{1,0:T(8,128)S(1)} collective-permute-done((f32[8,1024]{1,0:T(8,128)S(1)}, f32[8,1024]{1,0:T(8,128)S(1)}, u32[]{:S(2)}, u32[]{:S(2)}) %collective-permute-start.55) | collective-permute-done | bytes 32800 | tf_op jit(solution)/shard_map/ppermute | solution.py:27
  (434 shorter events, 264.1 us)
Async XLA Ops:
  5.5 47.6 %collective-permute-start.3 = (bf16[1024,512]{1,0:T(8,128)(2,1)S(1)}, bf16[1024,512]{1,0:T(8,128)(2,1)}, u32[]{:S(2)}, u32[]{:S(2)}) collective-permute-start(bf16[1024,512]{1,0:T(8,128)(2,1)S(1)} %bitcast.87), channel_id=1, source_target_pairs={{0,1},{1,0},{2,3},{3,2},{4,5},{5,4},{6,7},{7,6},{8,9},{9,8},{10,11... | collective-permute-start | bytes 3145736 | tf_op jit(solution)/shard_map/ppermute | solution.py:27
  5.5 45.7 %collective-permute-start.1 = (bf16[1024,512]{1,0:T(8,128)(2,1)S(1)}, bf16[1024,512]{1,0:T(8,128)(2,1)}, u32[]{:S(2)}, u32[]{:S(2)}) collective-permute-start(bf16[1024,512]{1,0:T(8,128)(2,1)S(1)} %bitcast.83), channel_id=1, source_target_pairs={{0,2},{1,3},{2,0},{3,1},{4,6},{5,7},{6,4},{7,5},{8,10},{9,11},{10,... | collective-permute-start | bytes 3145736 | tf_op jit(solution)/shard_map/ppermute | solution.py:27
  5.6 75.1 %collective-permute-start = (bf16[1024,512]{1,0:T(8,128)(2,1)S(1)}, bf16[1024,512]{1,0:T(8,128)(2,1)}, u32[]{:S(2)}, u32[]{:S(2)}) collective-permute-start(bf16[1024,512]{1,0:T(8,128)(2,1)S(1)} %bitcast.84), channel_id=1, source_target_pairs={{0,1},{1,0},{2,3},{3,2},{4,5},{5,4},{6,7},{7,6},{8,9},{9,8},{10,11... | collective-permute-start | bytes 3145736 | tf_op jit(solution)/shard_map/ppermute | solution.py:27
  174.9 69.5 %collective-permute-start.26 = (bf16[1024,512]{1,0:T(8,128)(2,1)S(1)}, bf16[1024,512]{1,0:T(8,128)(2,1)}, u32[]{:S(2)}, u32[]{:S(2)}) collective-permute-start(bf16[1024,512]{1,0:T(8,128)(2,1)S(1)} %bitcast.80), channel_id=1, source_target_pairs={{0,2},{1,3},{2,0},{3,1},{4,6},{5,7},{6,4},{7,5},{8,10},{9,11},{10,... | collective-permute-start | bytes 3145736 | tf_op jit(solution)/shard_map/ppermute | solution.py:27
  196.3 55.7 %collective-permute-start.25 = (bf16[1024,512]{1,0:T(8,128)(2,1)S(1)}, bf16[1024,512]{1,0:T(8,128)(2,1)}, u32[]{:S(2)}, u32[]{:S(2)}) collective-permute-start(bf16[1024,512]{1,0:T(8,128)(2,1)S(1)} %bitcast.81), channel_id=1, source_target_pairs={{0,1},{1,0},{2,3},{3,2},{4,5},{5,4},{6,7},{7,6},{8,9},{9,8},{10,11... | collective-permute-start | bytes 3145736 | tf_op jit(solution)/shard_map/ppermute | solution.py:27
  198.7 46.2 %collective-permute-start.8 = (bf16[1024,512]{1,0:T(8,128)(2,1)}, bf16[1024,512]{1,0:T(8,128)(2,1)}, u32[]{:S(2)}, u32[]{:S(2)}) collective-permute-start(bf16[1024,512]{1,0:T(8,128)(2,1)} %get-tuple-element.134), channel_id=1, source_target_pairs={{0,1},{1,0},{2,3},{3,2},{4,5},{5,4},{6,7},{7,6},{8,9},{9,8},{10,11... | collective-permute-start | bytes 3145736 | tf_op jit(solution)/shard_map/ppermute | solution.py:27
  199.0 45.9 %collective-permute-start.10 = (bf16[1024,512]{1,0:T(8,128)(2,1)S(1)}, bf16[1024,512]{1,0:T(8,128)(2,1)}, u32[]{:S(2)}, u32[]{:S(2)}) collective-permute-start(bf16[1024,512]{1,0:T(8,128)(2,1)S(1)} %add_convert_fusion.18), channel_id=1, source_target_pairs={{0,2},{1,3},{2,0},{3,1},{4,6},{5,7},{6,4},{7,5},{8,10},{9,11},{10,... | collective-permute-start | bytes 3145736 | tf_op jit(solution)/shard_map/ppermute | solution.py:27
  219.5 45.0 %collective-permute-start.23 = (bf16[1024,512]{1,0:T(8,128)(2,1)}, bf16[1024,512]{1,0:T(8,128)(2,1)}, u32[]{:S(2)}, u32[]{:S(2)}) collective-permute-start(bf16[1024,512]{1,0:T(8,128)(2,1)} %get-tuple-element.148.refs_0_), channel_id=1, source_target_pairs={{0,2},{1,3},{2,0},{3,1},{4,6},{5,7},{6,4},{7,5},{8,10},{9,11},{10,... | collective-permute-start | bytes 3145736 | tf_op jit(solution)/shard_map/ppermute | solution.py:27
  244.4 42.6 %collective-permute-start.15 = (bf16[1024,512]{1,0:T(8,128)(2,1)S(1)}, bf16[1024,512]{1,0:T(8,128)(2,1)}, u32[]{:S(2)}, u32[]{:S(2)}) collective-permute-start(bf16[1024,512]{1,0:T(8,128)(2,1)S(1)} %bitcast.77), channel_id=1, source_target_pairs={{0,2},{1,3},{2,0},{3,1},{4,6},{5,7},{6,4},{7,5},{8,10},{9,11},{10,... | collective-permute-start | bytes 3145736 | tf_op jit(solution)/shard_map/ppermute | solution.py:27
  245.0 42.1 %collective-permute-start.27 = (bf16[1024,512]{1,0:T(8,128)(2,1)}, bf16[1024,512]{1,0:T(8,128)(2,1)}, u32[]{:S(2)}, u32[]{:S(2)}) collective-permute-start(bf16[1024,512]{1,0:T(8,128)(2,1)} %collective-permute-done.26.refs_6_), channel_id=1, source_target_pairs={{0,1},{1,0},{2,3},{3,2},{4,5},{5,4},{6,7},{7,6},{8,9},{9,8},{10,11... | collective-permute-start | bytes 3145736 | tf_op jit(solution)/shard_map/ppermute | solution.py:27
  245.0 42.6 %collective-permute-start.22 = (bf16[1024,512]{1,0:T(8,128)(2,1)}, bf16[1024,512]{1,0:T(8,128)(2,1)}, u32[]{:S(2)}, u32[]{:S(2)}) collective-permute-start(bf16[1024,512]{1,0:T(8,128)(2,1)} %get-tuple-element.148.refs_0_), channel_id=1, source_target_pairs={{0,1},{1,0},{2,3},{3,2},{4,5},{5,4},{6,7},{7,6},{8,9},{9,8},{10,11... | collective-permute-start | bytes 3145736 | tf_op jit(solution)/shard_map/ppermute | solution.py:27
  252.0 56.6 %collective-permute-start.12 = (bf16[1024,512]{1,0:T(8,128)(2,1)}, bf16[1024,512]{1,0:T(8,128)(2,1)}, u32[]{:S(2)}, u32[]{:S(2)}) collective-permute-start(bf16[1024,512]{1,0:T(8,128)(2,1)} %get-tuple-element.138.refs_0_), channel_id=1, source_target_pairs={{0,2},{1,3},{2,0},{3,1},{4,6},{5,7},{6,4},{7,5},{8,10},{9,11},{10,... | collective-permute-start | bytes 3145736 | tf_op jit(solution)/shard_map/ppermute | solution.py:27
  264.6 44.0 %collective-permute-start.24 = (bf16[1024,512]{1,0:T(8,128)(2,1)}, bf16[1024,512]{1,0:T(8,128)(2,1)}, u32[]{:S(2)}, u32[]{:S(2)}) collective-permute-start(bf16[1024,512]{1,0:T(8,128)(2,1)} %collective-permute-done.23.refs_2_), channel_id=1, source_target_pairs={{0,1},{1,0},{2,3},{3,2},{4,5},{5,4},{6,7},{7,6},{8,9},{9,8},{10,11... | collective-permute-start | bytes 3145736 | tf_op jit(solution)/shard_map/ppermute | solution.py:27
  287.0 76.3 %collective-permute-start.14 = (bf16[1024,512]{1,0:T(8,128)(2,1)S(1)}, bf16[1024,512]{1,0:T(8,128)(2,1)}, u32[]{:S(2)}, u32[]{:S(2)}) collective-permute-start(bf16[1024,512]{1,0:T(8,128)(2,1)S(1)} %bitcast.78), channel_id=1, source_target_pairs={{0,1},{1,0},{2,3},{3,2},{4,5},{5,4},{6,7},{7,6},{8,9},{9,8},{10,11... | collective-permute-start | bytes 3145736 | tf_op jit(solution)/shard_map/ppermute | solution.py:27
  287.1 76.4 %collective-permute-start.16 = (bf16[1024,512]{1,0:T(8,128)(2,1)}, bf16[1024,512]{1,0:T(8,128)(2,1)}, u32[]{:S(2)}, u32[]{:S(2)}) collective-permute-start(bf16[1024,512]{1,0:T(8,128)(2,1)} %collective-permute-done.15.refs_6_), channel_id=1, source_target_pairs={{0,1},{1,0},{2,3},{3,2},{4,5},{5,4},{6,7},{7,6},{8,9},{9,8},{10,11... | collective-permute-start | bytes 3145736 | tf_op jit(solution)/shard_map/ppermute | solution.py:27
  287.6 75.8 %collective-permute-start.11 = (bf16[1024,512]{1,0:T(8,128)(2,1)S(1)}, bf16[1024,512]{1,0:T(8,128)(2,1)}, u32[]{:S(2)}, u32[]{:S(2)}) collective-permute-start(bf16[1024,512]{1,0:T(8,128)(2,1)S(1)} %copy-done.53), channel_id=1, source_target_pairs={{0,1},{1,0},{2,3},{3,2},{4,5},{5,4},{6,7},{7,6},{8,9},{9,8},{10,11... | collective-permute-start | bytes 3145736 | tf_op jit(solution)/shard_map/ppermute | solution.py:27
  308.6 54.8 %collective-permute-start.13 = (bf16[1024,512]{1,0:T(8,128)(2,1)}, bf16[1024,512]{1,0:T(8,128)(2,1)}, u32[]{:S(2)}, u32[]{:S(2)}) collective-permute-start(bf16[1024,512]{1,0:T(8,128)(2,1)} %collective-permute-done.12.refs_2_), channel_id=1, source_target_pairs={{0,1},{1,0},{2,3},{3,2},{4,5},{5,4},{6,7},{7,6},{8,9},{9,8},{10,11... | collective-permute-start | bytes 3145736 | tf_op jit(solution)/shard_map/ppermute | solution.py:27
  362.8 84.4 %collective-permute-start.32 = (bf16[1024,512]{1,0:T(8,128)(2,1)}, bf16[1024,512]{1,0:T(8,128)(2,1)S(1)}, u32[]{:S(2)}, u32[]{:S(2)}) collective-permute-start(bf16[1024,512]{1,0:T(8,128)(2,1)} %get-tuple-element.164), channel_id=1, source_target_pairs={{0,1},{1,0},{2,3},{3,2},{4,5},{5,4},{6,7},{7,6},{8,9},{9,8},{10,11... | collective-permute-start | bytes 3145736 | tf_op jit(solution)/shard_map/ppermute | solution.py:27
  363.3 137.2 %collective-permute-start.31 = (bf16[1024,512]{1,0:T(8,128)(2,1)}, bf16[1024,512]{1,0:T(8,128)(2,1)}, u32[]{:S(2)}, u32[]{:S(2)}) collective-permute-start(bf16[1024,512]{1,0:T(8,128)(2,1)} %get-tuple-element.162), channel_id=1, source_target_pairs={{0,1},{1,0},{2,3},{3,2},{4,5},{5,4},{6,7},{7,6},{8,9},{9,8},{10,11... | collective-permute-start | bytes 3145736 | tf_op jit(solution)/shard_map/ppermute | solution.py:27
  447.0 53.4 %collective-permute-start.28 = (bf16[1024,512]{1,0:T(8,128)(2,1)S(1)}, bf16[1024,512]{1,0:T(8,128)(2,1)S(1)}, u32[]{:S(2)}, u32[]{:S(2)}) collective-permute-start(bf16[1024,512]{1,0:T(8,128)(2,1)S(1)} %copy-done.54), channel_id=1, source_target_pairs={{0,1},{1,0},{2,3},{3,2},{4,5},{5,4},{6,7},{7,6},{8,9},{9,8},{10,11... | collective-permute-start | bytes 3145736 | tf_op jit(solution)/shard_map/ppermute | solution.py:27
  452.0 49.0 %collective-permute-start.33 = (bf16[1024,512]{1,0:T(8,128)(2,1)S(1)}, bf16[1024,512]{1,0:T(8,128)(2,1)S(1)}, u32[]{:S(2)}, u32[]{:S(2)}) collective-permute-start(bf16[1024,512]{1,0:T(8,128)(2,1)S(1)} %add_convert_fusion.15), channel_id=1, source_target_pairs={{0,2},{1,3},{2,0},{3,1},{4,6},{5,7},{6,4},{7,5},{8,10},{9,11},{10,... | collective-permute-start | bytes 3145736 | tf_op jit(solution)/shard_map/ppermute | solution.py:27
  453.4 49.1 %collective-permute-start.30 = (bf16[1024,512]{1,0:T(8,128)(2,1)S(1)}, bf16[1024,512]{1,0:T(8,128)(2,1)S(1)}, u32[]{:S(2)}, u32[]{:S(2)}) collective-permute-start(bf16[1024,512]{1,0:T(8,128)(2,1)S(1)} %add_convert_fusion.16), channel_id=1, source_target_pairs={{0,2},{1,3},{2,0},{3,1},{4,6},{5,7},{6,4},{7,5},{8,10},{9,11},{10,... | collective-permute-start | bytes 3145736 | tf_op jit(solution)/shard_map/ppermute | solution.py:27
  499.2 207.2 %collective-permute-start.85 = (bf16[1024,1408]{1,0:T(8,128)(2,1)}, bf16[1024,1408]{1,0:T(8,128)(2,1)S(1)}, u32[]{:S(2)}, u32[]{:S(2)}) collective-permute-start(bf16[1024,1408]{1,0:T(8,128)(2,1)} %convolution_convert_fusion), channel_id=1, source_target_pairs={{0,4},{4,0},{8,12},{12,8},{16,20},{20,16},{24,28},{28,24},{1,5},{5... | collective-permute-start | bytes 8650760 | tf_op jit(solution)/shard_map/ppermute | solution.py:27
  502.5 46.4 %collective-permute-start.48 = (bf16[1024,512]{1,0:T(8,128)(2,1)}, bf16[1024,512]{1,0:T(8,128)(2,1)}, u32[]{:S(2)}, u32[]{:S(2)}) collective-permute-start(bf16[1024,512]{1,0:T(8,128)(2,1)} %add_convert_fusion.13), channel_id=1, source_target_pairs={{0,2},{1,3},{2,0},{3,1},{4,6},{5,7},{6,4},{7,5},{8,10},{9,11},{10,... | collective-permute-start | bytes 3145736 | tf_op jit(solution)/shard_map/ppermute | solution.py:27
  527.6 190.2 %collective-permute-start.79 = (bf16[1024,1408]{1,0:T(8,128)(2,1)}, bf16[1024,1408]{1,0:T(8,128)(2,1)}, u32[]{:S(2)}, u32[]{:S(2)}) collective-permute-start(bf16[1024,1408]{1,0:T(8,128)(2,1)} %convolution_convert_fusion.4), channel_id=1, source_target_pairs={{0,4},{4,0},{8,12},{12,8},{16,20},{20,16},{24,28},{28,24},{1,5},{5... | collective-permute-start | bytes 8650760 | tf_op jit(solution)/shard_map/ppermute | solution.py:27
  528.4 194.1 %collective-permute-start.82 = (bf16[1024,1408]{1,0:T(8,128)(2,1)}, bf16[1024,1408]{1,0:T(8,128)(2,1)}, u32[]{:S(2)}, u32[]{:S(2)}) collective-permute-start(bf16[1024,1408]{1,0:T(8,128)(2,1)} %convolution_convert_fusion.2), channel_id=1, source_target_pairs={{0,4},{4,0},{8,12},{12,8},{16,20},{20,16},{24,28},{28,24},{1,5},{5... | collective-permute-start | bytes 8650760 | tf_op jit(solution)/shard_map/ppermute | solution.py:27
  548.9 140.2 %collective-permute-start.42 = (f32[8,1024]{1,0:T(8,128)}, f32[8,1024]{1,0:T(8,128)S(1)}, u32[]{:S(2)}, u32[]{:S(2)}) collective-permute-start(f32[8,1024]{1,0:T(8,128)} %get-tuple-element.181), channel_id=1, source_target_pairs={{0,1},{1,0},{2,3},{3,2},{4,5},{5,4},{6,7},{7,6},{8,9},{9,8},{10,11... | collective-permute-start | bytes 98312 | tf_op jit(solution)/shard_map/ppermute | solution.py:27
  560.0 125.6 %collective-permute-start.90 = (f32[3]{0:T(128)S(1)}, f32[3]{0:T(128)S(1)}, u32[]{:S(2)}, u32[]{:S(2)}) collective-permute-start(f32[3]{0:T(128)S(1)} %add.267), channel_id=1, source_target_pairs={{0,4},{4,0},{8,12},{12,8},{16,20},{20,16},{24,28},{28,24},{1,5},{5... | collective-permute-start | bytes 44 | tf_op jit(solution)/shard_map/ppermute | solution.py:27
  717.8 41.9 %collective-permute-start.86 = (bf16[512,1408]{1,0:T(8,128)(2,1)}, bf16[512,1408]{1,0:T(8,128)(2,1)}, u32[]{:S(2)}, u32[]{:S(2)}) collective-permute-start(bf16[512,1408]{1,0:T(8,128)(2,1)} %slice.213), channel_id=1, source_target_pairs={{0,8},{4,12},{8,0},{12,4},{16,24},{20,28},{24,16},{28,20},{1,9},{5... | collective-permute-start | bytes 4325384 | tf_op jit(solution)/shard_map/ppermute | solution.py:27
  722.4 79.3 %collective-permute-start.80 = (bf16[512,1408]{1,0:T(8,128)(2,1)}, bf16[512,1408]{1,0:T(8,128)(2,1)}, u32[]{:S(2)}, u32[]{:S(2)}) collective-permute-start(bf16[512,1408]{1,0:T(8,128)(2,1)} %slice.205), channel_id=1, source_target_pairs={{0,8},{4,12},{8,0},{12,4},{16,24},{20,28},{24,16},{28,20},{1,9},{5... | collective-permute-start | bytes 4325384 | tf_op jit(solution)/shard_map/ppermute | solution.py:27
  729.2 115.8 %collective-permute-start.83 = (bf16[512,1408]{1,0:T(8,128)(2,1)}, bf16[512,1408]{1,0:T(8,128)(2,1)}, u32[]{:S(2)}, u32[]{:S(2)}) collective-permute-start(bf16[512,1408]{1,0:T(8,128)(2,1)} %slice.209), channel_id=1, source_target_pairs={{0,8},{4,12},{8,0},{12,4},{16,24},{20,28},{24,16},{28,20},{1,9},{5... | collective-permute-start | bytes 4325384 | tf_op jit(solution)/shard_map/ppermute | solution.py:27
  741.9 183.3 %collective-permute-start.39 = (bf16[1024,512]{1,0:T(8,128)(2,1)}, bf16[1024,512]{1,0:T(8,128)(2,1)}, u32[]{:S(2)}, u32[]{:S(2)}) collective-permute-start(bf16[1024,512]{1,0:T(8,128)(2,1)} %get-tuple-element.178.refs_0_), channel_id=1, source_target_pairs={{0,1},{1,0},{2,3},{3,2},{4,5},{5,4},{6,7},{7,6},{8,9},{9,8},{10,11... | collective-permute-start | bytes 3145736 | tf_op jit(solution)/shard_map/ppermute | solution.py:27
  741.9 183.3 %collective-permute-start.41 = (bf16[1024,512]{1,0:T(8,128)(2,1)}, bf16[1024,512]{1,0:T(8,128)(2,1)}, u32[]{:S(2)}, u32[]{:S(2)}) collective-permute-start(bf16[1024,512]{1,0:T(8,128)(2,1)} %collective-permute-done.40.refs_2_), channel_id=1, source_target_pairs={{0,1},{1,0},{2,3},{3,2},{4,5},{5,4},{6,7},{7,6},{8,9},{9,8},{10,11... | collective-permute-start | bytes 3145736 | tf_op jit(solution)/shard_map/ppermute | solution.py:27
  756.2 93.4 %all-to-all-start.6 = ((bf16[8,2,128,128]{3,2,1,0:T(8,128)(2,1)}), bf16[8,2,128,128]{3,2,1,0:T(8,128)(2,1)S(1)}, u32[]{:S(2)}, u32[]{:S(2)}) async-start(bf16[8,2,128,128]{3,2,1,0:T(8,128)(2,1)} %bitcast.90), calls=%async_computation.6 | async-start | bytes 1048576 | tf_op jit(solution)/shard_map/all_to_all | solution.py:428
  761.7 86.7 %collective-permute-start.87 = (bf16[256,1408]{1,0:T(8,128)(2,1)S(1)}, bf16[256,1408]{1,0:T(8,128)(2,1)S(1)}, u32[]{:S(2)}, u32[]{:S(2)}) collective-permute-start(bf16[256,1408]{1,0:T(8,128)(2,1)S(1)} %slice.215), channel_id=1, source_target_pairs={{0,16},{4,20},{8,24},{12,28},{16,0},{20,4},{24,8},{28,12},{1,17},{... | collective-permute-start | bytes 2162696 | tf_op jit(solution)/shard_map/ppermute | solution.py:27
  804.4 77.8 %collective-permute-start.81 = (bf16[256,1408]{1,0:T(8,128)(2,1)}, bf16[256,1408]{1,0:T(8,128)(2,1)}, u32[]{:S(2)}, u32[]{:S(2)}) collective-permute-start(bf16[256,1408]{1,0:T(8,128)(2,1)} %slice.207), channel_id=1, source_target_pairs={{0,16},{4,20},{8,24},{12,28},{16,0},{20,4},{24,8},{28,12},{1,17},{... | collective-permute-start | bytes 2162696 | tf_op jit(solution)/shard_map/ppermute | solution.py:27
  847.6 49.8 %collective-permute-start.84 = (bf16[256,1408]{1,0:T(8,128)(2,1)}, bf16[256,1408]{1,0:T(8,128)(2,1)}, u32[]{:S(2)}, u32[]{:S(2)}) collective-permute-start(bf16[256,1408]{1,0:T(8,128)(2,1)} %slice.211), channel_id=1, source_target_pairs={{0,16},{4,20},{8,24},{12,28},{16,0},{20,4},{24,8},{28,12},{1,17},{... | collective-permute-start | bytes 2162696 | tf_op jit(solution)/shard_map/ppermute | solution.py:27
  852.4 50.4 %all-to-all-start.7 = ((bf16[8,2,128,128]{3,2,1,0:T(8,128)(2,1)}), bf16[8,2,128,128]{3,2,1,0:T(8,128)(2,1)S(1)}, u32[]{:S(2)}, u32[]{:S(2)}) async-start(bf16[8,2,128,128]{3,2,1,0:T(8,128)(2,1)} %scan_states.7), calls=%async_computation.7 | async-start | bytes 1048576 | tf_op jit(solution)/shard_map/all_to_all | solution.py:434
  945.3 63.0 %collective-permute-start.76 = (bf16[1024,512]{1,0:T(8,128)(2,1)}, bf16[1024,512]{1,0:T(8,128)(2,1)}, u32[]{:S(2)}, u32[]{:S(2)}) collective-permute-start(bf16[1024,512]{1,0:T(8,128)(2,1)} %convolution_convert_fusion.6), channel_id=1, source_target_pairs={{0,4},{4,0},{8,12},{12,8},{16,20},{20,16},{24,28},{28,24},{1,5},{5... | collective-permute-start | bytes 3145736 | tf_op jit(solution)/shard_map/ppermute | solution.py:27
  953.4 58.8 %collective-permute-start.73 = (bf16[1024,512]{1,0:T(8,128)(2,1)}, bf16[1024,512]{1,0:T(8,128)(2,1)}, u32[]{:S(2)}, u32[]{:S(2)}) collective-permute-start(bf16[1024,512]{1,0:T(8,128)(2,1)} %convolution_convert_fusion.8), channel_id=1, source_target_pairs={{0,4},{4,0},{8,12},{12,8},{16,20},{20,16},{24,28},{28,24},{1,5},{5... | collective-permute-start | bytes 3145736 | tf_op jit(solution)/shard_map/ppermute | solution.py:27
  954.1 46.9 %all-to-all-start.4 = ((bf16[8,2,128,128]{3,2,1,0:T(8,128)(2,1)}), bf16[8,2,128,128]{3,2,1,0:T(8,128)(2,1)S(1)}, u32[]{:S(2)}, u32[]{:S(2)}) async-start(bf16[8,2,128,128]{3,2,1,0:T(8,128)(2,1)} %bitcast.16), calls=%async_computation.4 | async-start | bytes 1048576 | tf_op jit(solution)/shard_map/all_to_all | solution.py:428
  967.4 52.7 %collective-permute-start.64 = (bf16[1024,512]{1,0:T(8,128)(2,1)}, bf16[1024,512]{1,0:T(8,128)(2,1)}, u32[]{:S(2)}, u32[]{:S(2)}) collective-permute-start(bf16[1024,512]{1,0:T(8,128)(2,1)} %convolution_convert_fusion.14), channel_id=1, source_target_pairs={{0,4},{4,0},{8,12},{12,8},{16,20},{20,16},{24,28},{28,24},{1,5},{5... | collective-permute-start | bytes 3145736 | tf_op jit(solution)/shard_map/ppermute | solution.py:27
  969.3 52.7 %collective-permute-start.62 = (bf16[1024,512]{1,0:T(8,128)(2,1)}, bf16[1024,512]{1,0:T(8,128)(2,1)S(1)}, u32[]{:S(2)}, u32[]{:S(2)}) collective-permute-start(bf16[1024,512]{1,0:T(8,128)(2,1)} %get-tuple-element.223), channel_id=1, source_target_pairs={{0,1},{1,0},{2,3},{3,2},{4,5},{5,4},{6,7},{7,6},{8,9},{9,8},{10,11... | collective-permute-start | bytes 3145736 | tf_op jit(solution)/shard_map/ppermute | solution.py:27
  973.5 141.9 %collective-permute-start.61 = (bf16[1024,512]{1,0:T(8,128)(2,1)}, bf16[1024,512]{1,0:T(8,128)(2,1)}, u32[]{:S(2)}, u32[]{:S(2)}) collective-permute-start(bf16[1024,512]{1,0:T(8,128)(2,1)} %get-tuple-element.221), channel_id=1, source_target_pairs={{0,1},{1,0},{2,3},{3,2},{4,5},{5,4},{6,7},{7,6},{8,9},{9,8},{10,11... | collective-permute-start | bytes 3145736 | tf_op jit(solution)/shard_map/ppermute | solution.py:27
  1003.8 46.1 %all-to-all-start.5 = ((bf16[8,2,128,128]{3,2,1,0:T(8,128)(2,1)}), bf16[8,2,128,128]{3,2,1,0:T(8,128)(2,1)}, u32[]{:S(2)}, u32[]{:S(2)}) async-start(bf16[8,2,128,128]{3,2,1,0:T(8,128)(2,1)} %scan_states.6), calls=%async_computation.5 | async-start | bytes 1048576 | tf_op jit(solution)/shard_map/all_to_all | solution.py:434
  1035.0 51.2 %collective-permute-start.78 = (bf16[256,512]{1,0:T(8,128)(2,1)}, bf16[256,512]{1,0:T(8,128)(2,1)}, u32[]{:S(2)}, u32[]{:S(2)}) collective-permute-start(bf16[256,512]{1,0:T(8,128)(2,1)} %slice.203), channel_id=1, source_target_pairs={{0,16},{4,20},{8,24},{12,28},{16,0},{20,4},{24,8},{28,12},{1,17},{... | collective-permute-start | bytes 786440 | tf_op jit(solution)/shard_map/ppermute | solution.py:27
  1040.6 46.7 %collective-permute-start.75 = (bf16[256,512]{1,0:T(8,128)(2,1)}, bf16[256,512]{1,0:T(8,128)(2,1)}, u32[]{:S(2)}, u32[]{:S(2)}) collective-permute-start(bf16[256,512]{1,0:T(8,128)(2,1)} %slice.199), channel_id=1, source_target_pairs={{0,16},{4,20},{8,24},{12,28},{16,0},{20,4},{24,8},{28,12},{1,17},{... | collective-permute-start | bytes 786440 | tf_op jit(solution)/shard_map/ppermute | solution.py:27
  1089.7 54.7 %collective-permute-start.63 = (bf16[1024,512]{1,0:T(8,128)(2,1)S(1)}, bf16[1024,512]{1,0:T(8,128)(2,1)}, u32[]{:S(2)}, u32[]{:S(2)}) collective-permute-start(bf16[1024,512]{1,0:T(8,128)(2,1)S(1)} %add_convert_fusion.11), channel_id=1, source_target_pairs={{0,2},{1,3},{2,0},{3,1},{4,6},{5,7},{6,4},{7,5},{8,10},{9,11},{10,... | collective-permute-start | bytes 3145736 | tf_op jit(solution)/shard_map/ppermute | solution.py:27
  (125 other events, 1937.6 us)
